TPU v7x, 768 devices: a whole 4x8x12 slice. The times are simulated.
768 devices in a mesh: shard: 12 (over z), group: 64 (over x, y, core).
Axes of the slice: x: 4, y: 8, z: 12, core: 2. Of those that a mesh axis runs over, the one named last changes fastest.
Arguments:
- item_ids: int32 [98304], P(('shard', 'group')), may hold values from 0 to 8191, as said below
- seq_lengths: int32 [768, 8], P(('shard', 'group')), may hold values from 1 to 64, 128 in all within a row
- time_buckets: int32 [98304], P(('shard', 'group')), may hold values from 0 to 63
- neg_ids: int32 [12, 2048], P('shard', 'group'), may hold values from 0 to 8191, as said below
- table: float32 [8192, 512], P('group'), may hold values from -6 to 6
- w_in: float32 [512, 2048], replicated, may hold values from -0.25 to 0.25
- b_in: float32 [2048], replicated, may hold values from -3 to 3
- w_out: float32 [512, 512], replicated, may hold values from -0.25 to 0.25
- rab: float32 [4, 64], replicated, may hold values from -4 to 4
Outputs:
- table_grad: float32 [8192, 512], P('group')
- token_loss: float32 [98304], P(('shard', 'group'))
Inputs may be any that keep to these rules, and one draw needn't show every extreme that they name: `item_ids`: item i is held by the rows of group index i // 128. The 128 tokens of one device name items of any one group index at most 4 times; in every draw, for each shard index, one group index is named exactly 4 times by every device of that shard index. `neg_ids`: entry r of a row names an item of group index r // 32.
All inputs are finite; a program needn't handle non-finite values.
Results may differ from a plain program's by a relative error of at most 0.0003.
Values sent between devices are 32-bit elements; how exact they have to be, the bound alone decides.
A program may use at most 64 MiB of HBM per device.

v0:
```python
import jax
import jax.numpy as jnp
from jax import lax
from jax.sharding import PartitionSpec as P

MOST_LEN = 64


HIGH = lax.Precision.HIGHEST
TEMPER = 0.05


def layer_norm(value):
    mean = jnp.mean(value, -1, keepdims=True)
    centered = value - mean
    var = jnp.mean(centered * centered, -1, keepdims=True)
    return centered * lax.rsqrt(var + 1e-05)


def unit(value):
    return value * lax.rsqrt(jnp.sum(value * value, -1, keepdims=True) + 1e-06)


def time_bias(buckets, rab):
    nbuck = rab.shape[1]
    levels = jnp.arange(nbuck, dtype=jnp.int32)
    gapgrid = jnp.abs(levels[:, None] - levels[None, :])
    gap_hot = (gapgrid[:, :, None] == levels[None, None, :]).astype(jnp.float32)
    pair_bias = jnp.einsum("nmd,hd->hnm", gap_hot, rab, precision=HIGH)
    token_hot = (buckets[:, None] == levels[None, :]).astype(jnp.float32)
    left = jnp.einsum("in,hnm->him", token_hot, pair_bias, precision=HIGH)
    return jnp.einsum("him,jm->hij", left, token_hot, precision=HIGH)


def hstu(emb, buckets, segment, w_in, b_in, w_out, rab):
    count = emb.shape[0]
    heads = rab.shape[0]
    hidden = jax.nn.silu(
        jnp.dot(layer_norm(emb), w_in, precision=HIGH, preferred_element_type=jnp.float32) + b_in
    )
    upart, vpart, qpart, kpart = jnp.split(hidden, 4, axis=1)
    qpart = qpart.reshape(count, heads, -1)
    kpart = kpart.reshape(count, heads, -1)
    vpart = vpart.reshape(count, heads, -1)
    scores = jnp.einsum("ihd,jhd->hij", qpart, kpart, precision=HIGH) * qpart.shape[2] ** (-0.5)
    scores = scores + time_bias(buckets, rab)
    places = jnp.arange(count, dtype=jnp.int32)
    allowed = (places[None, :] <= places[:, None]) & (segment[None, :] == segment[:, None])
    weights = jax.nn.silu(scores) * allowed.astype(jnp.float32) / MOST_LEN
    mixed = jnp.einsum("hij,jhd->ihd", weights, vpart, precision=HIGH).reshape(count, -1)
    return (
        jnp.dot(
            layer_norm(mixed) * upart, w_out, precision=HIGH, preferred_element_type=jnp.float32
        )
        + emb
    )


def picker_of(wanted, rows_dev):
    flat = wanted.reshape(-1)
    return (flat[:, None] == jnp.arange(rows_dev, dtype=jnp.int32)[None, :]).astype(jnp.float32)


def body(item_ids, seq_lengths, time_buckets, neg_ids, table, w_in, b_in, w_out, rab):
    groups = lax.axis_size("group")
    rows_dev = table.shape[0]
    width = table.shape[1]
    count = item_ids.shape[0]
    capacity = max(2, 2 * count // groups)
    slots = groups * capacity
    owner = item_ids // rows_dev
    local_row = item_ids % rows_dev
    member = (owner[:, None] == jnp.arange(groups, dtype=jnp.int32)[None, :]).astype(jnp.int32)
    rank = jnp.sum(member * (jnp.cumsum(member, 0) - 1), 1)
    target_slot = owner * capacity + rank
    requests = (
        jnp.full((slots,), -1, jnp.int32).at[target_slot].set(local_row).reshape(groups, capacity)
    )
    own_negatives = unit(table[neg_ids.reshape(-1) % rows_dev])
    panel_rows = lax.all_gather(own_negatives, "group", axis=0, tiled=True)
    incoming = lax.all_to_all(requests, "group", split_axis=0, concat_axis=0, tiled=True)
    picker = picker_of(incoming, rows_dev)
    served = jnp.dot(picker, table, precision=HIGH, preferred_element_type=jnp.float32).reshape(
        groups, capacity, width
    )
    returned = lax.all_to_all(served, "group", split_axis=0, concat_axis=0, tiled=True).reshape(
        slots, width
    )
    emb = returned[target_slot]
    lengths = seq_lengths.reshape(-1)
    ends = jnp.cumsum(lengths)
    places = jnp.arange(count, dtype=jnp.int32)
    segment = jnp.sum((places[:, None] >= ends[None, :]).astype(jnp.int32), 1)
    following = jnp.concatenate([segment[1:], jnp.full((1,), -1, jnp.int32)])
    valid = (following == segment).astype(jnp.float32)

    def states_of(inputs):
        states = unit(hstu(inputs, time_buckets, segment, w_in, b_in, w_out, rab))
        shifted = jnp.concatenate([inputs[1:], jnp.zeros((1, width), jnp.float32)])
        return (states, unit(shifted))

    (states, target), back = jax.vjp(states_of, emb)
    exps = jnp.exp(
        jnp.dot(states, panel_rows.T, precision=HIGH, preferred_element_type=jnp.float32) / TEMPER
    )
    zneg = jnp.sum(exps, 1)
    pulled = jnp.dot(exps, panel_rows, precision=HIGH, preferred_element_type=jnp.float32)
    positive = jnp.sum(states * target, -1) / TEMPER
    expos = jnp.exp(positive)
    total = expos + zneg
    token_loss = valid * (jnp.log(total) - positive)
    share = expos / total - 1.0
    d_states = valid[:, None] * (share[:, None] * target + pulled / total[:, None]) / TEMPER
    d_target = valid[:, None] * (share[:, None] * states) / TEMPER
    d_emb = back((d_states, d_target))[0]
    outgoing = (
        jnp.zeros((slots, width), jnp.float32)
        .at[target_slot]
        .set(d_emb)
        .reshape(groups, capacity, width)
    )
    arrived = lax.all_to_all(outgoing, "group", split_axis=0, concat_axis=0, tiled=True).reshape(
        slots, width
    )
    partial_grad = jnp.dot(picker.T, arrived, precision=HIGH, preferred_element_type=jnp.float32)
    table_grad = lax.psum(partial_grad, "shard")
    return (table_grad, token_loss)


def solution(mesh):
    in_specs = (
        P(("shard", "group")),
        P(("shard", "group"), None),
        P(("shard", "group")),
        P("shard", "group"),
        P("group", None),
        P(),
        P(),
        P(),
        P(),
    )
    out_specs = (P("group", None), P(("shard", "group")))
    return jax.shard_map(body, mesh=mesh, in_specs=in_specs, out_specs=out_specs, check_vma=False)
```

profile of v0, /device:TPU:2, one launch (start us, length us, event | category | flops | bytes accessed | tf_op | source)
XLA Modules:
  0.0 278.6 jit_solution(4747965431943960380)
XLA Ops:
  8.0 1.6 gather_fusion.1
  11.6 1.0 scatter_custom_fusion
  13.3 13.7 %all-to-all-start = ((s32[64,1,4]{2,1,0:T(1,128)}), s32[64,1,4]{2,1,0:T(1,128)S(1)}, u32[]{:S(2)}, u32[]{:S(2)}) async-start(s32[64,1,4]{2,1,0:T(1,128)} %bitcast), calls=%async_computation | async-start | bytes 65536 | tf_op jit(solution)/shard_map/all_to_all | solution.py:81
  28.6 6.9 %all-to-all-done = s32[64,1,4]{2,1,0:T(1,128)S(1)} async-done(((s32[64,1,4]{2,1,0:T(1,128)}), s32[64,1,4]{2,1,0:T(1,128)S(1)}, u32[]{:S(2)}, u32[]{:S(2)}) %all-to-all-start) | async-done | bytes 1056 | tf_op jit(solution)/shard_map/all_to_all | solution.py:81
  36.8 1.4 fusion.50
  38.2 0.9 reshape.309
  39.2 5.5 %all-to-all-start.1 = ((f32[64,4,512]{2,1,0:T(4,128)}), f32[64,4,512]{2,1,0:T(4,128)S(1)}, u32[]{:S(2)}, u32[]{:S(2)}) async-start(f32[64,4,512]{2,1,0:T(4,128)} %reshape.309), calls=%async_computation.1 | async-start | bytes 1048576 | tf_op jit(solution)/shard_map/all_to_all | solution.py:86
  46.2 2.9 %fusion.4 = f32[4,64,64]{2,0,1:T(4,128)S(1)} fusion(s32[64,64]{1,0:T(8,128)S(1)} %subtract_abs_fusion, f32[4,64]{1,0:T(4,128)S(1)} %copy-done.21), kind=kOutput, calls=%fused_computation.17 | convolution fusion | flops 12845056 | bytes 82944 | tf_op jit(solution)/shard_map/jvp(nmd,hd->hnm)/dot_general | solution.py:29
  49.4 13.1 %all-to-all-done.1 = f32[64,4,512]{2,1,0:T(4,128)S(1)} async-done(((f32[64,4,512]{2,1,0:T(4,128)}), f32[64,4,512]{2,1,0:T(4,128)S(1)}, u32[]{:S(2)}, u32[]{:S(2)}) %all-to-all-start.1) | async-done | bytes 524320 | tf_op jit(solution)/shard_map/all_to_all | solution.py:86
  63.8 5.5 %fusion.12 = (f32[128,2048]{1,0:T(8,128)S(1)}, f32[128,2048]{1,0:T(8,128)}) fusion(f32[2048]{0:T(1024)S(1)} %copy-done.13, f32[512,2048]{1,0:T(8,128)} %param.14, f32[128,512]{1,0:T(8,128)S(1)} %gather_fusion, f32[128]{0:T(128)S(1)} %fusion.67, f32[128]{0:T(128)S(1)} %broadcast_multiply_fusion.5), kind=kOutput, calls=%fused_computation.27 | convolution fusion | flops 1612054528 | bytes 6562816 | tf_op jit(solution)/shard_map/jvp()/dot_general | solution.py:39
  71.0 1.0 convolution_add_fusion.1
  72.1 2.4 fusion.75
  74.5 1.1 copy.64
  75.8 1.0 fusion.22
  77.9 30.3 %all-gather.2.cloned.1.call-done = f32[2048,512]{1,0:T(8,128)} async-done(((f32[32,512]{1,0:T(8,128)}), f32[2048,512]{1,0:T(8,128)}) %all-gather.2.cloned.1.call-update) | async-done | bytes 4194320 | tf_op jit(solution)/shard_map/all_gather | solution.py:80
  108.2 6.8 %fusion.76 = (f32[128]{0:T(128)S(1)}, f32[128,2048]{1,0:T(8,128)S(1)}) fusion(f32[2048,512]{1,0:T(8,128)} %all-gather.2.cloned.1.call-done, f32[128,512]{1,0:T(8,128)S(1)} %get-tuple-element.27, f32[128]{0:T(128)S(1)} %get-tuple-element.36), kind=kOutput, calls=%fused_computation.153 | convolution fusion | flops 1611202432 | bytes 5506048 | tf_op jit(solution)/shard_map/dot_general | solution.py:104
  115.7 3.4 %multiply_reduce_fusion.3 = (f32[128]{0:T(128)S(1)}, f32[128,512]{1,0:T(8,128)}, f32[128]{0:T(128)S(1)}, f32[128,512]{1,0:T(8,128)S(1)}) fusion(f32[127,512]{1,0:T(8,128)S(1)} %slice.12, f32[128,512]{1,0:T(8,128)S(1)} %get-tuple-element.27, f32[128]{0:T(128)S(1)} %get-tuple-element.36, f32[128]{0:T(128)S(1)} %get-tuple-element.14, f32[128]{0:T(128)S(1)} %copy-done.14, ...), kind=kOutput, calls=%fused_computation.57 | convolution fusion | flops 1611529984 | bytes 6292992 | tf_op jit(solution)/shard_map/dot_general | solution.py:107
  119.1 1.3 multiply_reduce_fusion.1
  125.0 7.2 %multiply_reduce_fusion = (f32[128]{0:T(128)S(1)}, f32[128,512]{1,0:T(8,128)S(1)}) fusion(f32[128,512]{1,0:T(8,128)S(1)} %gather_fusion, f32[128]{0:T(128)S(1)} %broadcast_multiply_fusion.5, f32[512,2048]{1,0:T(8,128)} %param.14, f32[128,2048]{1,0:T(8,128)} %get-tuple-element.23, f32[128,512]{1,0:T(8,128)} %copy.69, f32[128,512]{1,0:T(8,128)S(1)} %copy.68, ...), kind=kOutput, calls=%fused_computation.51 | convolution fusion | flops 1613954944 | bytes 6816768 | tf_op jit(solution)/shard_map/transpose(jvp())/dot_general | solution.py:39
  132.5 1.4 scatter_custom_fusion.1
  134.1 24.4 %all_to_all.19 = f32[64,4,512]{2,1,0:T(4,128)S(1)} all-to-all(f32[64,4,512]{2,1,0:T(4,128)S(1)} %reshape.320), channel_id=1, replica_groups=mesh['shard'=12,'group'=64] {'group'}, dimensions={0} | all-to-all | bytes 1048576 | tf_op jit(solution)/shard_map/all_to_all | solution.py:122
  158.7 1.1 fusion.49
  159.8 110.3 %all-reduce.4.cloned.1.call-done = f32[128,512]{1,0:T(8,128)} async-done(((f32[128,512]{1,0:T(8,128)}), f32[128,512]{1,0:T(8,128)}) %all-reduce.4.cloned.1.call-update) | async-done | bytes 262160 | tf_op jit(solution)/shard_map/psum | solution.py:126
  270.0 1.7 copy.95
  (107 shorter events, 18.0 us)
Async XLA Ops:
  7.2 69.6 %copy-start = (f32[512,512]{1,0:T(8,128)S(1)}, f32[512,512]{1,0:T(8,128)}, u32[]{:S(2)}) copy-start(f32[512,512]{1,0:T(8,128)} %param.16) | copy-start | bytes 3145732
  7.2 39.0 %copy-start.21 = (f32[4,64]{1,0:T(4,128)S(1)}, f32[4,64]{1,0:T(4,128)}, u32[]{:S(2)}) copy-start(f32[4,64]{1,0:T(4,128)} %param.17) | copy-start | bytes 3076
  7.2 41.9 %copy-start.17 = (s32[128]{0:T(128)S(1)}, s32[128]{0:T(128)}, u32[]{:S(2)}) copy-start(s32[128]{0:T(128)} %param.11) | copy-start | bytes 1540
  7.2 101.0 %all-gather.2.cloned.1.call-start = ((), (), s32[]{:S(2)}) async-start(), calls=%async_computation.3 | async-start | bytes 4259840 | tf_op jit(solution)/shard_map/all_gather | solution.py:80
  11.5 52.2 %copy-start.20 = (s32[128]{0:T(128)}, s32[128]{0:T(128)S(1)}, u32[]{:S(2)}) copy-start(s32[128]{0:T(128)S(1)} %compare_select_fusion.1) | copy-start | bytes 1540
  13.3 22.2 %all-to-all-start = ((s32[64,1,4]{2,1,0:T(1,128)}), s32[64,1,4]{2,1,0:T(1,128)S(1)}, u32[]{:S(2)}, u32[]{:S(2)}) async-start(s32[64,1,4]{2,1,0:T(1,128)} %bitcast), calls=%async_computation | async-start | bytes 65536 | tf_op jit(solution)/shard_map/all_to_all | solution.py:81
  27.9 7.5 %copy-start.15 = (s32[127]{0:T(128)}, s32[127]{0:T(128)S(1)}, u32[]{:S(2)}) copy-start(s32[127]{0:T(128)S(1)} %slice.6) | copy-start | bytes 1528
  36.8 27.0 %copy-start.13 = (f32[2048]{0:T(1024)S(1)}, f32[2048]{0:T(1024)}, u32[]{:S(2)}) copy-start(f32[2048]{0:T(1024)} %param.15) | copy-start | bytes 24580
  39.2 23.3 %all-to-all-start.1 = ((f32[64,4,512]{2,1,0:T(4,128)}), f32[64,4,512]{2,1,0:T(4,128)S(1)}, u32[]{:S(2)}, u32[]{:S(2)}) async-start(f32[64,4,512]{2,1,0:T(4,128)} %reshape.309), calls=%async_computation.1 | async-start | bytes 1048576 | tf_op jit(solution)/shard_map/all_to_all | solution.py:86
  44.7 225.4 %all-reduce.4.cloned.1.call-start = ((), (), s32[]{:S(2)}) async-start(), calls=%async_computation.4 | async-start | bytes 524288 | tf_op jit(solution)/shard_map/psum | solution.py:126
  63.8 5.6 %copy-start.18 = (f32[128]{0:T(128)}, f32[128]{0:T(128)S(1)}, u32[]{:S(2)}) copy-start(f32[128]{0:T(128)S(1)} %multiply_reduce_fusion.7) | copy-start | bytes 1540
  70.4 6.4 %copy-start.2 = (f32[128,512]{0,1:T(8,128)}, f32[128,512]{0,1:T(8,128)S(1)}, u32[]{:S(2)}) copy-start(f32[128,512]{0,1:T(8,128)S(1)} %copy.71) | copy-start | bytes 786436
  75.7 39.3 %copy-start.16 = (s32[127]{0:T(128)S(1)}, s32[127]{0:T(128)}, u32[]{:S(2)}) copy-start(s32[127]{0:T(128)} %copy-done.15) | copy-start | bytes 1528
  75.8 39.9 %copy-start.14 = (f32[128]{0:T(128)S(1)}, f32[128]{0:T(128)}, u32[]{:S(2)}) copy-start(f32[128]{0:T(128)} %fusion.71) | copy-start | bytes 1540
  108.2 7.4 %copy-start.1 = (f32[2048,512]{1,0:T(8,128)S(1)}, f32[2048,512]{1,0:T(8,128)}, u32[]{:S(2)}) copy-start(f32[2048,512]{1,0:T(8,128)} %all-gather.2.cloned.1.call-done) | copy-start | bytes 12582916
  115.6 5.7 %copy-start.9 = (f32[4,128,128]{2,1,0:T(8,128)S(1)}, f32[4,128,128]{2,1,0:T(8,128)}, u32[]{:S(2)}) copy-start(f32[4,128,128]{2,1,0:T(8,128)} %copy-done.8) | copy-start | bytes 786436
  115.6 5.7 %copy-start.12 = (f32[128,128]{1,0:T(8,128)S(1)}, f32[128,128]{1,0:T(8,128)}, u32[]{:S(2)}) copy-start(f32[128,128]{1,0:T(8,128)} %fusion.56) | copy-start | bytes 196612
  115.6 6.3 %copy-start.10 = (f32[16,4,8,128]{3,2,1,0:T(8,128)S(1)}, f32[16,4,8,128]{3,2,1,0:T(8,128)}, u32[]{:S(2)}) copy-start(f32[16,4,8,128]{3,2,1,0:T(8,128)} %get-tuple-element.8) | copy-start | bytes 786436
  115.6 6.3 %copy-start.11 = (f32[128,128]{1,0:T(8,128)S(1)}, f32[128,128]{1,0:T(8,128)}, u32[]{:S(2)}) copy-start(f32[128,128]{1,0:T(8,128)} %fusion.55) | copy-start | bytes 196612
  119.1 4.7 %copy-start.4 = (f32[128,512]{1,0:T(8,128)}, f32[128,512]{1,0:T(8,128)S(1)}, u32[]{:S(2)}) copy-start(f32[128,512]{1,0:T(8,128)S(1)} %get-tuple-element.30) | copy-start | bytes 786436
  121.3 3.7 %copy-start.7 = (f32[128,512]{1,0:T(8,128)S(1)}, f32[128,512]{1,0:T(8,128)}, u32[]{:S(2)}) copy-start(f32[128,512]{1,0:T(8,128)} %get-tuple-element.11) | copy-start | bytes 786436
  124.9 7.2 %copy-start.19 = (f32[128]{0:T(128)S(1)}, f32[128]{0:T(128)}, u32[]{:S(2)}) copy-start(f32[128]{0:T(128)} %copy-done.18) | copy-start | bytes 1540
  124.9 7.4 %copy-start.6 = (f32[128,512]{1,0:T(8,128)S(1)}, f32[128,512]{1,0:T(8,128)}, u32[]{:S(2)}) copy-start(f32[128,512]{1,0:T(8,128)} %get-tuple-element.5) | copy-start | bytes 786436
  124.9 7.5 %copy-start.5 = (f32[128,512]{1,0:T(8,128)S(1)}, f32[128,512]{1,0:T(8,128)}, u32[]{:S(2)}) copy-start(f32[128,512]{1,0:T(8,128)} %copy-done.4) | copy-start | bytes 786436
  (2 other events, 6.1 us)
Sparse Core Ops, SparseCore 0:
  12.0 96.1 all-gather.1
  159.9 110.0 all-reduce.3
where the time goes:
time: 279 us
  waiting for transfers between devices  161 us (58%)
  matrix products  37.3 us (13%)
  blocking collectives  24.4 us (9%)
  starting transfers between devices  19.3 us (7%)
  between operations  14.5 us (5%)
  local copies, waits for them, and re-layouts  11.2 us (4%)
  other arithmetic  11.2 us (4%)
    psum x1, waiting for transfers between devices, body(): table_grad = lax.psum(partial_grad, 'shard')  110 us
    all_gather x1, waiting for transfers between devices, body(): panel_rows = lax.all_gather(own_negatives, 'group', axis=0, tiled=True)  30.3 us
    all_to_all x1, blocking collectives, body(): lax.all_to_all(outgoing, 'group', split_axis=0, concat_axis=0, tiled=True)  24.4 us
    all_to_all x1, starting transfers between devices, body(): lax.all_to_all(requests, 'group', split_axis=0, concat_axis=0, tiled=True)  13.7 us
    all_to_all x1, waiting for transfers between devices, body(): lax.all_to_all(served, 'group', split_axis=0, concat_axis=0, tiled=True)  13.1 us
    dot_general x2, matrix products, hstu(): jnp.dot(layer_norm(emb), w_in, precision=HIGH, preferred_element_type=jnp...  12.7 us
    all_to_all x1, waiting for transfers between devices, body(): lax.all_to_all(requests, 'group', split_axis=0, concat_axis=0, tiled=True)  6.89 us
    dot_general x1, matrix products, body(): jnp.dot(states, panel_rows.T, precision=HIGH, preferred_element_type=jnp....  6.84 us
  transfers between devices with their start and end apart: 4, of which 4 were waited for; matrix products, arithmetic and copies ran while one was open for 10% of the time, Pallas kernels for 0%

commit v1 on v0

--- a/solution.py
+++ b/solution.py
@@ -1,14 +1,381 @@
+import functools
+
 import jax
 import jax.numpy as jnp
 from jax import lax
+from jax.experimental import pallas as pl
+from jax.experimental.pallas import tpu as pltpu
 from jax.sharding import PartitionSpec as P
 
 MOST_LEN = 64
 
 
-HIGH = lax.Precision.HIGHEST
+HIGH = lax.Precision.HIGH
 TEMPER = 0.05
-
+MESH = pl.DeviceIdType.MESH
+F32 = jnp.float32
+BF16 = jnp.bfloat16
+
+
+def pieces_of(value, count):
+    terms = []
+    for _ in range(count):
+        term = value.astype(BF16)
+        terms.append(term)
+        value = value - term.astype(F32)
+    return terms
+
+
+def select_dot(onehot, value, count=3):
+    return sum(jnp.dot(onehot, term, preferred_element_type=F32) for term in pieces_of(value, count))
+
+
+def iota(shape, dim):
+    return lax.broadcasted_iota(jnp.int32, shape, dim)
+
+
+def hot(mask):
+    return mask.astype(F32).astype(BF16)
+
+
+def greet(sem, device):
+    pl.semaphore_signal(sem, inc=1, device_id=device, device_id_type=MESH)
+
+
+def remote(src, dst, send_sem, recv_sem, device):
+    return pltpu.make_async_remote_copy(
+        src_ref=src, dst_ref=dst, send_sem=send_sem, recv_sem=recv_sem, device_id=device, device_id_type=MESH
+    )
+
+
+def rows8(index, rows=8):
+    return pl.ds(pl.multiple_of(index * rows, rows), rows)
+
+
+def fetch_kernel(
+    dims, ids_ref, neg_ref, table_ref, emb_ref, panel_ref, place_ref, picks_ref,
+    req_out, req_in, expand, served, recv, req_sems, row_sems, neg_send, neg_recv,
+):
+    nx, ny = dims
+    groups = nx * ny * 2
+    count = ids_ref.shape[1]
+    nneg = neg_ref.shape[1]
+    slots = groups * 8
+    me = lax.axis_index("group")
+    core = lax.rem(me, 2)
+    x, y = me // (2 * ny), lax.rem(me // 2, ny)
+
+    def at(xx, yy, cc):
+        return (lax.rem(xx + nx, nx) * ny + lax.rem(yy + ny, ny)) * 2 + cc
+
+    barrier = pltpu.get_barrier_semaphore()
+
+    def hello(k, c):
+        greet(barrier, {"group": lax.rem(me + k, groups)})
+        return c
+
+    lax.fori_loop(1, groups, hello, 0)
+
+    ids = jnp.broadcast_to(ids_ref[...], (count, count))
+    ids_t = ids.T
+    rows_dev = table_ref.shape[0]
+    own_row, own_col = ids // rows_dev, ids_t // rows_dev
+    same = own_row == own_col
+    col, row = iota((count, count), 1), iota((count, count), 0)
+    rank_col = jnp.sum(jnp.where(same & (col < row), 1, 0), axis=1, keepdims=True)
+    rank_row = jnp.sum(jnp.where(same & (row < col), 1, 0), axis=0, keepdims=True)
+    slot_col = own_col[:, :1] * 8 + rank_col
+    slot_row = own_row[:1] * 8 + rank_row
+    owner_hot = hot(jnp.broadcast_to(own_row[:1], (groups, count)) == iota((groups, count), 0))
+    wanted = jnp.where(lax.rem(col, 4) == rank_col, ids_t - own_col * rows_dev + 1, 0)
+    requests = jnp.dot(owner_hot, wanted.astype(F32).astype(BF16), preferred_element_type=F32)
+    for g in range(groups):
+        req_out[g] = requests[g : g + 1].astype(jnp.int32)
+    neg_row = lax.rem(neg_ref[...], rows_dev)
+    neg_hot = hot(jnp.broadcast_to(neg_row, (rows_dev, nneg)) == iota((rows_dev, nneg), 0)).T
+    drawn = select_dot(neg_hot, table_ref[...])
+    mine = rows8(me, nneg)
+    panel_ref[mine] = drawn * lax.rsqrt(jnp.sum(drawn * drawn, -1, keepdims=True) + 1e-06)
+    pl.semaphore_wait(barrier, groups - 1)
+
+    def ask(k, c):
+        peer = lax.rem(me + k, groups)
+        remote(req_out.at[peer], req_in.at[me], req_sems.at[0], req_sems.at[1], {"group": peer}).start()
+        return c
+
+    lax.fori_loop(1, groups, ask, 0)
+    req_in[me] = req_out[me]
+
+    def pass_on(block, device):
+        where = rows8(block, nneg)
+        remote(panel_ref.at[where], panel_ref.at[where], neg_send, neg_recv.at[block], {"group": device}).start()
+
+    def arrive(block):
+        where = rows8(block, nneg)
+        remote(panel_ref.at[where], panel_ref.at[where], neg_send, neg_recv.at[block], {"group": me}).wait_recv()
+
+    sibling = at(x, y, 1 - core)
+
+    def along_y(block, up, down):
+        if up:
+            pass_on(block, at(x, y + 1, core))
+        if down:
+            pass_on(block, at(x, y - 1, core))
+        pass_on(block, at(x + 1, y, core))
+        pass_on(block, at(x - 1, y, core))
+        pass_on(block, sibling)
+
+    ups, downs = ny // 2, (ny - 1) // 2
+    along_y(me, True, True)
+
+    def asked():
+        return remote(
+            req_out.at[pl.ds(0, groups - 1)], req_in.at[pl.ds(0, groups - 1)], req_sems.at[0], req_sems.at[1], {"group": me}
+        )
+
+    asked().wait_recv()
+
+    def widen(g, c):
+        expand[rows8(g)] = jnp.broadcast_to(req_in[g], (8, count))
+        return c
+
+    lax.fori_loop(0, groups, widen, 0)
+    lanes, subs = iota((slots, count), 1), lax.rem(iota((slots, count), 0), 8)
+    kept = jnp.where(lanes == lax.rem(subs, 4), expand[...], 0).astype(F32).astype(BF16)
+    ones = jnp.ones((count, count), BF16)
+    named = jnp.dot(kept, ones, preferred_element_type=F32).astype(jnp.int32)
+    named_t = lax.dot_general(ones, kept, (((1,), (1,)), ((), ())), preferred_element_type=F32).astype(jnp.int32)
+    fits = named == lanes + 1
+    serve = jnp.concatenate([hot(fits & (subs < 4)), hot(fits & (subs >= 4))], axis=1)
+    half = table_ref.shape[1] // 2
+    stacked = jnp.concatenate([table_ref[:, :half], table_ref[:, half:]], axis=0)
+    served[...] = select_dot(serve, stacked)
+
+    def give(k, c):
+        peer = lax.rem(me + k, groups)
+        remote(served.at[rows8(peer)], recv.at[rows8(me)], row_sems.at[0], row_sems.at[1], {"group": peer}).start()
+        return c
+
+    lax.fori_loop(1, groups, give, 0)
+    recv[rows8(me)] = served[rows8(me)]
+    fits_t = named_t == iota((count, slots), 0) + 1
+    subs_t = lax.rem(iota((count, slots), 1), 8)
+    picks_ref[0] = hot(fits_t & (subs_t < 4))
+    picks_ref[1] = hot(fits_t & (subs_t >= 4))
+    slot_sub = iota((slots, count), 0)
+    place_ref[:, :count] = hot(slot_sub == slot_row)
+    place_ref[:, count:] = hot(slot_sub == slot_row + 4)
+
+    for k in range(1, ups + 1):
+        block = at(x, y - k, core)
+        arrive(block)
+        along_y(block, k < ups, False)
+        if k <= downs:
+            block = at(x, y + k, core)
+            arrive(block)
+            along_y(block, False, k < downs)
+    order = [0] + [s * k for k in range(1, ups + 1) for s in (-1, 1) if s < 0 or k <= downs]
+    for dy in order:
+        for dx in (-1, 1):
+            block = at(x + dx, y + dy, core)
+            arrive(block)
+            if (dy % 2 == 0) == (dx < 0):
+                pass_on(block, at(x - dx, y, core))
+            pass_on(block, sibling)
+    for dy in order:
+        block = at(x + 2, y + dy, core)
+        arrive(block)
+        pass_on(block, sibling)
+
+    def given():
+        return remote(
+            served.at[pl.ds(0, (groups - 1) * 8)], recv.at[pl.ds(0, (groups - 1) * 8)], row_sems.at[0], row_sems.at[1],
+            {"group": me},
+        )
+
+    given().wait_recv()
+    slot_lane = iota((count, slots), 1)
+    for q in range(2):
+        emb_ref[:, q * half : (q + 1) * half] = select_dot(hot(slot_lane == slot_col + 4 * q), recv[...])
+    for dx in range(nx):
+        for dy in range(ny):
+            arrive(at(x + dx, y + dy, 1 - core))
+    asked().wait_send()
+    given().wait_send()
+    sent = pl.ds(0, (groups - 1) * nneg)
+    remote(panel_ref.at[sent], panel_ref.at[sent], neg_send, neg_recv.at[0], {"group": me}).wait_send()
+
+
+def fetch(dims, ids, negs, table):
+    groups = dims[0] * dims[1] * 2
+    count, width, nneg = ids.shape[1], table.shape[1], negs.shape[1]
+    slots = groups * 8
+    vm = pl.BlockSpec(memory_space=pltpu.VMEM)
+    shape = jax.ShapeDtypeStruct
+    return pl.pallas_call(
+        functools.partial(fetch_kernel, dims),
+        out_shape=(
+            shape((count, width), F32),
+            shape((groups * nneg, width), F32),
+            shape((slots, 2 * count), BF16),
+            shape((2, count, slots), BF16),
+        ),
+        in_specs=[vm] * 3,
+        out_specs=(vm,) * 4,
+        scratch_shapes=[
+            pltpu.VMEM((groups, 1, count), jnp.int32),
+            pltpu.VMEM((groups, 1, count), jnp.int32),
+            pltpu.VMEM((slots, count), jnp.int32),
+            pltpu.VMEM((slots, width // 2), F32),
+            pltpu.VMEM((slots, width // 2), F32),
+            pltpu.SemaphoreType.DMA((2,)),
+            pltpu.SemaphoreType.DMA((2,)),
+            pltpu.SemaphoreType.DMA,
+            pltpu.SemaphoreType.DMA((groups,)),
+        ],
+        compiler_params=pltpu.CompilerParams(collective_id=0, has_side_effects=True, vmem_limit_bytes=48 << 20),
+        name="fetch",
+    )(ids, negs, table)
+
+def grad_kernel(
+    G, S, piece, grad_ref, place_ref, pick_ref, red_ref, out_ref, recv, part, rs, send_sem, recv_sem, rs_send, rs_recv, ag_send, ag_recv,
+):
+    me = lax.axis_index("group")
+    my = lax.axis_index("shard")
+    barrier = pltpu.get_barrier_semaphore()
+
+    def greet(k, c):
+        pl.semaphore_signal(barrier, inc=1, device_id={"group": lax.rem(me + k, G)}, device_id_type=MESH)
+        return c
+
+    lax.fori_loop(1, G, greet, 0)
+
+    def greet_s(k, c):
+        pl.semaphore_signal(barrier, inc=1, device_id={"shard": lax.rem(my + k, S)}, device_id_type=MESH)
+        return c
+
+    lax.fori_loop(1, S, greet_s, 0)
+    chunks = out_ref.shape[0]
+    for h in range(chunks):
+        stacked = jnp.concatenate([grad_ref[:, (2 * h + q) * 128 : (2 * h + q + 1) * 128] for q in range(2)], axis=0)
+        out_ref[h] = select_dot(place_ref[...], stacked)
+    pl.semaphore_wait(barrier, G - 1 + S - 1)
+    for h in range(chunks):
+
+        def send(k, c):
+            peer = lax.rem(me + k, G)
+            pltpu.make_async_remote_copy(
+                src_ref=out_ref.at[h, pl.ds(pl.multiple_of(peer * 8, 8), 8)],
+                dst_ref=recv.at[h, pl.ds(pl.multiple_of(me * 8, 8), 8)],
+                send_sem=send_sem.at[h],
+                recv_sem=recv_sem.at[h],
+                device_id={"group": peer},
+                device_id_type=MESH,
+            ).start()
+            return c
+
+        lax.fori_loop(1, G, send, 0)
+        own = pl.ds(pl.multiple_of(me * 8, 8), 8)
+        recv[h, own] = out_ref[h, own]
+
+    def whole(h):
+        return pltpu.make_async_remote_copy(
+            src_ref=out_ref.at[h, pl.ds(0, (G - 1) * 8)],
+            dst_ref=recv.at[h, pl.ds(0, (G - 1) * 8)],
+            send_sem=send_sem.at[h],
+            recv_sem=recv_sem.at[h],
+            device_id={"group": me},
+            device_id_type=MESH,
+        )
+
+    half = 256
+    for h in range(chunks):
+        whole(h).wait_recv()
+        part[h, pl.ds(half, part.shape[1] - half)] = jnp.zeros((part.shape[1] - half, 128), F32)
+        for q in range(2):
+            part[h, pl.ds(q * 128, 128)] = select_dot(pick_ref[q], recv[h])
+
+        def scatter(k, c):
+            peer = lax.rem(my + k, S)
+            pltpu.make_async_remote_copy(
+                src_ref=part.at[h, pl.ds(pl.multiple_of(peer * piece, 8), piece)],
+                dst_ref=rs.at[h, my],
+                send_sem=rs_send.at[h],
+                recv_sem=rs_recv.at[h],
+                device_id={"shard": peer},
+                device_id_type=MESH,
+            ).start()
+            return c
+
+        lax.fori_loop(1, S, scatter, 0)
+        rs[h, my] = part[h, pl.ds(pl.multiple_of(my * piece, 8), piece)]
+
+    def whole_rs(h):
+        return pltpu.make_async_remote_copy(
+            src_ref=rs.at[h, pl.ds(0, S - 1)],
+            dst_ref=rs.at[h, pl.ds(0, S - 1)],
+            send_sem=rs_send.at[h],
+            recv_sem=rs_recv.at[h],
+            device_id={"shard": my},
+            device_id_type=MESH,
+        )
+
+    mine = pl.ds(pl.multiple_of(my * piece, 8), piece)
+    for h in range(chunks):
+        whole_rs(h).wait_recv()
+        red_ref[h, mine] = jnp.sum(rs[h], axis=0)
+
+        def spread(k, c):
+            peer = lax.rem(my + k, S)
+            pltpu.make_async_remote_copy(
+                src_ref=red_ref.at[h, mine],
+                dst_ref=red_ref.at[h, mine],
+                send_sem=ag_send.at[h],
+                recv_sem=ag_recv.at[h],
+                device_id={"shard": peer},
+                device_id_type=MESH,
+            ).start()
+            return c
+
+        lax.fori_loop(1, S, spread, 0)
+    for h in range(chunks):
+        tail = pltpu.make_async_remote_copy(
+            src_ref=red_ref.at[h, pl.ds(0, (S - 1) * piece)],
+            dst_ref=red_ref.at[h, pl.ds(0, (S - 1) * piece)],
+            send_sem=ag_send.at[h],
+            recv_sem=ag_recv.at[h],
+            device_id={"shard": my},
+            device_id_type=MESH,
+        )
+        tail.wait_recv()
+        tail.wait_send()
+        whole(h).wait_send()
+        whole_rs(h).wait_send()
+
+
+def exchange_grads(grads, place, picks, G, S):
+    count, width = grads.shape
+    chunks, slots = width // 256, place.shape[0]
+    piece = (-(-256 // S) + 7) // 8 * 8
+    rows = S * piece
+    vm = pl.BlockSpec(memory_space=pltpu.VMEM)
+    red = pl.pallas_call(
+        functools.partial(grad_kernel, G, S, piece),
+        out_shape=jax.ShapeDtypeStruct((chunks, rows, 128), F32),
+        in_specs=[vm] * 3,
+        out_specs=vm,
+        scratch_shapes=[
+            pltpu.VMEM((chunks, slots, 128), F32),
+            pltpu.VMEM((chunks, slots, 128), F32),
+            pltpu.VMEM((chunks, rows, 128), F32),
+            pltpu.VMEM((chunks, S, piece, 128), F32),
+        ]
+        + [pltpu.SemaphoreType.DMA((chunks,))] * 6,
+        compiler_params=pltpu.CompilerParams(collective_id=1, has_side_effects=True, vmem_limit_bytes=48 << 20),
+        name="grad_exchange",
+    )(grads, place, picks)
+    parts = red[:, :256].reshape(chunks * 2, count, 128)
+    return parts.transpose(1, 0, 2).reshape(count, width)
 
 def layer_norm(value):
     mean = jnp.mean(value, -1, keepdims=True)
@@ -56,37 +423,11 @@
     )
 
 
-def picker_of(wanted, rows_dev):
-    flat = wanted.reshape(-1)
-    return (flat[:, None] == jnp.arange(rows_dev, dtype=jnp.int32)[None, :]).astype(jnp.float32)
-
-
 def body(item_ids, seq_lengths, time_buckets, neg_ids, table, w_in, b_in, w_out, rab):
-    groups = lax.axis_size("group")
-    rows_dev = table.shape[0]
+    groups, shards = lax.axis_size("group"), lax.axis_size("shard")
     width = table.shape[1]
     count = item_ids.shape[0]
-    capacity = max(2, 2 * count // groups)
-    slots = groups * capacity
-    owner = item_ids // rows_dev
-    local_row = item_ids % rows_dev
-    member = (owner[:, None] == jnp.arange(groups, dtype=jnp.int32)[None, :]).astype(jnp.int32)
-    rank = jnp.sum(member * (jnp.cumsum(member, 0) - 1), 1)
-    target_slot = owner * capacity + rank
-    requests = (
-        jnp.full((slots,), -1, jnp.int32).at[target_slot].set(local_row).reshape(groups, capacity)
-    )
-    own_negatives = unit(table[neg_ids.reshape(-1) % rows_dev])
-    panel_rows = lax.all_gather(own_negatives, "group", axis=0, tiled=True)
-    incoming = lax.all_to_all(requests, "group", split_axis=0, concat_axis=0, tiled=True)
-    picker = picker_of(incoming, rows_dev)
-    served = jnp.dot(picker, table, precision=HIGH, preferred_element_type=jnp.float32).reshape(
-        groups, capacity, width
-    )
-    returned = lax.all_to_all(served, "group", split_axis=0, concat_axis=0, tiled=True).reshape(
-        slots, width
-    )
-    emb = returned[target_slot]
+    emb, panel_rows, place, picks = fetch((groups // 16, 8), item_ids.reshape(1, -1), neg_ids, table)
     lengths = seq_lengths.reshape(-1)
     ends = jnp.cumsum(lengths)
     places = jnp.arange(count, dtype=jnp.int32)
@@ -113,17 +454,7 @@
     d_states = valid[:, None] * (share[:, None] * target + pulled / total[:, None]) / TEMPER
     d_target = valid[:, None] * (share[:, None] * states) / TEMPER
     d_emb = back((d_states, d_target))[0]
-    outgoing = (
-        jnp.zeros((slots, width), jnp.float32)
-        .at[target_slot]
-        .set(d_emb)
-        .reshape(groups, capacity, width)
-    )
-    arrived = lax.all_to_all(outgoing, "group", split_axis=0, concat_axis=0, tiled=True).reshape(
-        slots, width
-    )
-    partial_grad = jnp.dot(picker.T, arrived, precision=HIGH, preferred_element_type=jnp.float32)
-    table_grad = lax.psum(partial_grad, "shard")
+    table_grad = exchange_grads(d_emb, place, picks, groups, shards)
     return (table_grad, token_loss)
 
 

time: 279 us -> 143 us (0.51)
  the two profiles are of different devices: /device:TPU:2 before, /device:TPU:1 now
where the time goes in v1:
time: 143 us; the launch traced here: 142 us
  Pallas kernels  98.5 us (69%)
  matrix products  27.4 us (19%)
  local copies, waits for them, and re-layouts  11.5 us (8%)
  other arithmetic  3.88 us (3%)
    pallas_call x1, Pallas kernels, fetch(): pl.pallas_call(functools.partial(fetch_kernel, dims), out_shape=(shape((c...  52.7 us
    pallas_call x1, Pallas kernels, exchange_grads(): pl.pallas_call(functools.partial(grad_kernel, G, S, piece), out_shape=jax...  45.8 us
    dot_general x2, matrix products, hstu(): jnp.dot(layer_norm(emb), w_in, precision=HIGH, preferred_element_type=jnp...  9.67 us
    unnamed x37, local copies, waits for them, and re-layouts  6.49 us
    dot_general x1, matrix products, body(): jnp.dot(states, panel_rows.T, precision=HIGH, preferred_element_type=jnp....  4.87 us
    dot_general x3, matrix products, hstu(): jnp.einsum('hij,jhd->ihd', weights, vpart, precision=HIGH)  3.54 us
    dot_general x3, matrix products, hstu(): jnp.einsum('ihd,jhd->hij', qpart, kpart, precision=HIGH)  2.94 us

profile of v1, /device:TPU:1, one launch (start us, length us, event | category | flops | bytes accessed | tf_op | source)
XLA Modules:
  0.0 142.3 jit_solution(560922104789200712)
XLA Ops:
  0.7 1.0 copy-done.3
  3.0 52.7 %fetch.1 = (f32[128,512]{1,0:T(8,128)S(1)}, f32[2048,512]{1,0:T(8,128)S(1)}, bf16[512,256]{1,0:T(8,128)(2,1)S(1)}, bf16[2,128,512]{2,1,0:T(8,128)(2,1)S(1)}) custom-call(s32[1,128]{1,0:T(1,128)S(1)} %bitcast.88, s32[1,32]{1,0:T(1,128)S(1)} %copy-done.5, f32[128,512]{1,0:T(8,128)S(1)} %copy-done.3), custom_call_target="tpu_custom_call" | custom-call | tf_op jit(solution)/shard_map/fetch/pallas_call | solution.py:215
  55.7 1.9 %copy-done.1 = f32[2048,512]{1,0:T(8,128)} copy-done((f32[2048,512]{1,0:T(8,128)}, f32[2048,512]{1,0:T(8,128)S(1)}, u32[]{:S(2)}) %copy-start.1) | copy-done | bytes 4194328
  58.0 4.6 %fusion.11 = (f32[128,2048]{1,0:T(8,128)S(1)}, f32[128,2048]{1,0:T(8,128)}) fusion(f32[2048]{0:T(1024)} %param.15, f32[512,2048]{1,0:T(8,128)} %param.14, f32[128,512]{1,0:T(8,128)S(1)} %get-tuple-element.6, f32[128]{0:T(128)S(1)} %fusion.51, f32[128]{0:T(128)S(1)} %broadcast_multiply_fusion.4), kind=kOutput, calls=%fused_computation.22 | convolution fusion | flops 806748160 | bytes 6562816 | tf_op jit(solution)/shard_map/jvp()/dot_general | solution.py:406
  62.6 0.9 slice_bitcast_fusion
  63.6 1.2 copy.46
  65.2 2.1 %fusion.1 = f32[64,64,4]{1,2,0:T(4,128)S(1)} fusion(s32[64,64]{1,0:T(8,128)S(1)} %subtract_abs_fusion, f32[4,64]{1,0:T(4,128)S(1)} %copy-done.16), kind=kOutput, calls=%fused_computation.4 | convolution fusion | flops 6553600 | bytes 82944 | tf_op jit(solution)/shard_map/jvp(nmd,hd->hnm)/dot_general | solution.py:396
  67.6 1.0 convolution_add_fusion.1
  69.0 1.5 %fusion.59 = (f32[128]{0:T(128)S(1)}, f32[4,128,128]{2,1,0:T(8,128)S(1)}) fusion(f32[4,128,128]{2,1,0:T(8,128)} %convolution_add_fusion.1, f32[128,128]{1,0:T(8,128)S(1)} %fusion.44, f32[16,4,8,128]{3,2,1,0:T(8,128)} %get-tuple-element.16), kind=kOutput, calls=%fused_computation.116 | convolution fusion | flops 50790272 | bytes 852480 | tf_op jit(solution)/shard_map/jvp(hij,jhd->ihd)/dot_general | solution.py:417
  71.2 1.1 copy.39
  73.0 4.9 %fusion.60 = (f32[128]{0:T(128)S(1)}, f32[128,2048]{1,0:T(8,128)S(1)}) fusion(f32[2048,512]{1,0:T(8,128)} %copy-done.1, f32[128,512]{1,0:T(8,128)S(1)} %get-tuple-element.33, f32[128]{0:T(128)S(1)} %get-tuple-element.42), kind=kOutput, calls=%fused_computation.117 | convolution fusion | flops 805896064 | bytes 5506048 | tf_op jit(solution)/shard_map/dot_general | solution.py:445
  78.8 1.7 %multiply_reduce_fusion.3 = (f32[128]{0:T(128)S(1)}, f32[128,512]{1,0:T(8,128)S(1)}, f32[128]{0:T(128)S(1)}, f32[128,512]{1,0:T(8,128)S(1)}) fusion(f32[127,512]{1,0:T(8,128)S(1)} %slice.10, f32[128,512]{1,0:T(8,128)S(1)} %get-tuple-element.33, f32[128]{0:T(128)S(1)} %get-tuple-element.42, f32[128]{0:T(128)S(1)} %get-tuple-element.22, f32[128]{0:T(128)S(1)} %fusion.55, ...), kind=kOutput, calls=%fused_computation.49 | convolution fusion | flops 806223616 | bytes 6292992 | tf_op jit(solution)/shard_map/dot_general | solution.py:448
  80.6 0.8 add_add_fusion.3
  81.4 0.8 multiply_reduce_fusion.1
  82.2 0.9 fusion.58
  83.0 0.7 copy-done.13
  84.4 1.6 %fusion.15 = f32[4,128,128]{2,1,0:T(8,128)S(1)} fusion(f32[4,128,128]{2,1,0:T(8,128)} %convolution_add_fusion.1, f32[16,4,8,128]{3,2,1,0:T(8,128)} %get-tuple-element.16, f32[128,128]{1,0:T(8,128)S(1)} %fusion.43, f32[128,512]{1,0:T(8,128)} %copy-done.13, f32[128]{0:T(128)S(1)} %negate_multiply_fusion.1), kind=kOutput, calls=%fused_computation.31 | convolution fusion | flops 51118080 | bytes 1114624 | tf_op jit(solution)/shard_map/transpose(jvp(hij,jhd->ihd))/dot_general | solution.py:417
  86.0 1.3 fusion.61
  87.4 0.8 copy.43
  88.2 1.2 fusion.62
  89.4 0.8 copy.44
  90.3 5.1 %multiply_reduce_fusion = (f32[128]{0:T(128)S(1)}, f32[128,512]{1,0:T(8,128)S(1)}) fusion(f32[128,512]{1,0:T(8,128)S(1)} %get-tuple-element.6, f32[128]{0:T(128)S(1)} %broadcast_multiply_fusion.4, f32[512,2048]{1,0:T(8,128)} %param.14, f32[128,2048]{1,0:T(8,128)} %get-tuple-element.29, f32[128,512]{1,0:T(8,128)} %copy.44, f32[128,512]{1,0:T(8,128)} %copy.43, ...), kind=kOutput, calls=%fused_computation.45 | convolution fusion | flops 808648576 | bytes 6816768 | tf_op jit(solution)/shard_map/transpose(jvp())/dot_general | solution.py:406
  95.7 45.8 %grad_exchange.1 = f32[2,288,128]{2,1,0:T(8,128)S(1)} custom-call(f32[128,512]{1,0:T(8,128)S(1)} %add_add_fusion.4.grad_ref, bf16[512,256]{1,0:T(8,128)(2,1)S(1)} %get-tuple-element.8.place_ref, bf16[2,128,512]{2,1,0:T(8,128)(2,1)S(1)} %get-tuple-element.9.pick_ref), custom_call_target="tpu_custom_call" | custom-call | tf_op jit(solution)/shard_map/grad_exchange/pallas_call | solution.py:362
  141.5 0.7 copy.73
  (67 shorter events, 6.2 us)
Async XLA Ops:
  0.6 71.6 %copy-start = (f32[512,512]{1,0:T(8,128)S(1)}, f32[512,512]{1,0:T(8,128)}, u32[]{:S(2)}) copy-start(f32[512,512]{1,0:T(8,128)} %param.16) | copy-start | bytes 3145732
  0.6 1.0 copy-start.3
  1.7 0.7 copy-start.4
  2.3 0.7 copy-start.5
  55.7 1.9 %copy-start.1 = (f32[2048,512]{1,0:T(8,128)}, f32[2048,512]{1,0:T(8,128)S(1)}, u32[]{:S(2)}) copy-start(f32[2048,512]{1,0:T(8,128)S(1)} %get-tuple-element.7) | copy-start | bytes 12582916
  57.9 7.3 %copy-start.16 = (f32[4,64]{1,0:T(4,128)S(1)}, f32[4,64]{1,0:T(4,128)}, u32[]{:S(2)}) copy-start(f32[4,64]{1,0:T(4,128)} %param.17) | copy-start | bytes 3076
  57.9 9.4 %copy-start.15 = (s32[128]{0:T(128)S(1)}, s32[128]{0:T(128)}, u32[]{:S(2)}) copy-start(s32[128]{0:T(128)} %param.11) | copy-start | bytes 1540
  57.9 10.7 %copy-start.17 = (s32[1,8]{1,0:T(1,128)S(1)}, s32[1,8]{1,0:T(1,128)}, u32[]{:S(2)}) copy-start(s32[1,8]{1,0:T(1,128)} %param.10) | copy-start | bytes 100
  63.6 7.6 %copy-start.6 = (f32[128,512]{0,1:T(8,128)}, f32[128,512]{0,1:T(8,128)S(1)}, u32[]{:S(2)}) copy-start(f32[128,512]{0,1:T(8,128)S(1)} %copy.45) | copy-start | bytes 786436
  64.8 5.8 %copy-start.7 = (f32[128,512]{0,1:T(8,128)}, f32[128,512]{0,1:T(8,128)S(1)}, u32[]{:S(2)}) copy-start(f32[128,512]{0,1:T(8,128)S(1)} %copy.46) | copy-start | bytes 786436
  70.5 0.7 copy-start.10
  72.3 6.5 %copy-start.2 = (f32[2048,512]{1,0:T(8,128)S(1)}, f32[2048,512]{1,0:T(8,128)}, u32[]{:S(2)}) copy-start(f32[2048,512]{1,0:T(8,128)} %copy-done.1) | copy-start | bytes 12582916
  78.8 4.9 %copy-start.14 = (f32[4,128,128]{2,1,0:T(8,128)S(1)}, f32[4,128,128]{2,1,0:T(8,128)}, u32[]{:S(2)}) copy-start(f32[4,128,128]{2,1,0:T(8,128)} %convolution_add_fusion.1) | copy-start | bytes 786436
  80.5 2.5 %copy-start.8 = (f32[128,512]{1,0:T(8,128)}, f32[128,512]{1,0:T(8,128)S(1)}, u32[]{:S(2)}) copy-start(f32[128,512]{1,0:T(8,128)S(1)} %get-tuple-element.36) | copy-start | bytes 786436
  83.0 0.7 copy-start.13
  83.0 7.2 %copy-start.12 = (f32[128,512]{1,0:T(8,128)S(1)}, f32[128,512]{1,0:T(8,128)}, u32[]{:S(2)}) copy-start(f32[128,512]{1,0:T(8,128)} %get-tuple-element.19) | copy-start | bytes 786436
  90.3 5.3 %copy-start.9 = (f32[128,512]{1,0:T(8,128)S(1)}, f32[128,512]{1,0:T(8,128)}, u32[]{:S(2)}) copy-start(f32[128,512]{1,0:T(8,128)} %copy-done.8) | copy-start | bytes 786436
  90.3 5.3 %copy-start.11 = (f32[127,512]{1,0:T(8,128)S(1)}, f32[127,512]{1,0:T(8,128)}, u32[]{:S(2)}) copy-start(f32[127,512]{1,0:T(8,128)} %add_add_fusion.3) | copy-start | bytes 780292

commit v2 on v0

v2 whole, which is shorter than its diff:
```python
import functools

import jax
import jax.numpy as jnp
from jax import lax
from jax.experimental import pallas as pl
from jax.experimental.pallas import tpu as pltpu
from jax.sharding import PartitionSpec as P

MOST_LEN = 64
TEMPER = 0.05
MESH = pl.DeviceIdType.MESH
F32 = jnp.float32
BF16 = jnp.bfloat16


def pieces_of(value, count):
    terms = []
    for _ in range(count):
        term = value.astype(BF16)
        terms.append(term)
        value = value - term.astype(F32)
    return terms


def select_dot(onehot, value, count=3):
    return sum(jnp.dot(onehot, term, preferred_element_type=F32) for term in pieces_of(value, count))


def iota(shape, dim):
    return lax.broadcasted_iota(jnp.int32, shape, dim)


def hot(mask):
    return mask.astype(F32).astype(BF16)


def greet(sem, device):
    pl.semaphore_signal(sem, inc=1, device_id=device, device_id_type=MESH)


def remote(src, dst, send_sem, recv_sem, device):
    return pltpu.make_async_remote_copy(
        src_ref=src, dst_ref=dst, send_sem=send_sem, recv_sem=recv_sem, device_id=device, device_id_type=MESH
    )


def rows8(index, rows=8):
    return pl.ds(pl.multiple_of(index * rows, rows), rows)


def weights_of(value):
    high = value.astype(BF16)
    return high, (value - high.astype(F32)).astype(BF16)


NN = (((1,), (0,)), ((), ()))
NT = (((1,), (1,)), ((), ()))


def mul3(left, high, low, dims=NN):
    count = left.shape[0]
    lhigh, llow = weights_of(left)
    both = lax.dot_general(jnp.concatenate([lhigh, llow], axis=0), high, dims, preferred_element_type=F32)
    return both[:count] + both[count:] + lax.dot_general(lhigh, low, dims, preferred_element_type=F32)


def rows_sum(value):
    return jnp.sum(value, axis=-1, keepdims=True)


def norm_back(d_norm, norm, scale):
    width = norm.shape[-1]
    return scale * (d_norm - rows_sum(d_norm) / width - norm * (rows_sum(d_norm * norm) / width))


def step_kernel(
    dims, shards, piece, heads,
    ids_h, len_h, time_h, neg_h, table_h, w_in_h, b_in_h, w_out_h, rab_h,
    red_ref, loss_ref,
    ids_v, len_s, time_v, neg_v, table_v, w_in_v, b_in_v, w_out_v, rab_s, load_sems,
    in_hi, in_lo, out_hi, out_lo, panel,
    req_out, req_in, expand, served, recv, place, picks,
    emb, norm, hid, slope, gap, bias, attn, attn_slope, mixed, dhid,
    outgoing, incoming, part, rsum,
    req_sems, row_sems, neg_send, neg_recv, send_sem, recv_sem, rs_send, rs_recv, ag_send, ag_recv,
):
    nx, ny = dims
    groups = nx * ny * 2
    count = ids_v.shape[1]
    width = table_v.shape[1]
    nneg = neg_v.shape[1]
    slots = groups * 8
    me, my = lax.axis_index("group"), lax.axis_index("shard")
    core = lax.rem(me, 2)
    x, y = me // (2 * ny), lax.rem(me // 2, ny)

    def at(xx, yy, cc):
        return (lax.rem(xx + nx, nx) * ny + lax.rem(yy + ny, ny)) * 2 + cc

    barrier = pltpu.get_barrier_semaphore()
    pairs = [
        (ids_h, ids_v), (table_h, table_v), (neg_h, neg_v), (len_h, len_s), (time_h, time_v), (rab_h, rab_s),
        (w_in_h, w_in_v), (w_out_h, w_out_v), (b_in_h, b_in_v),
    ]
    loads = [pltpu.make_async_copy(a, b, load_sems.at[i]) for i, (a, b) in enumerate(pairs)]
    for load in loads:
        load.start()

    def hello(k, c):
        greet(barrier, {"group": lax.rem(me + k, groups)})
        return c

    lax.fori_loop(1, groups, hello, 0)

    def hello_z(k, c):
        greet(barrier, {"shard": lax.rem(my + k, shards)})
        return c

    lax.fori_loop(1, shards, hello_z, 0)
    loads[0].wait()
    ids = jnp.broadcast_to(ids_v[...], (count, count))
    ids_t = ids.T
    rows_dev = table_v.shape[0]
    own_row, own_col = ids // rows_dev, ids_t // rows_dev
    same = own_row == own_col
    col, row = iota((count, count), 1), iota((count, count), 0)
    rank_col = jnp.sum(jnp.where(same & (col < row), 1, 0), axis=1, keepdims=True)
    rank_row = jnp.sum(jnp.where(same & (row < col), 1, 0), axis=0, keepdims=True)
    slot_col = own_col[:, :1] * 8 + rank_col
    slot_row = own_row[:1] * 8 + rank_row
    owner_hot = hot(jnp.broadcast_to(own_row[:1], (groups, count)) == iota((groups, count), 0))
    wanted = jnp.where(lax.rem(col, 4) == rank_col, ids_t - own_col * rows_dev + 1, 0)
    requests = jnp.dot(owner_hot, wanted.astype(F32).astype(BF16), preferred_element_type=F32)
    for g in range(groups):
        req_out[g] = requests[g : g + 1].astype(jnp.int32)
    loads[1].wait()
    loads[2].wait()
    pl.semaphore_wait(barrier, groups - 1 + shards - 1)

    def ask(k, c):
        peer = lax.rem(me + k, groups)
        remote(req_out.at[peer], req_in.at[me], req_sems.at[0], req_sems.at[1], {"group": peer}).start()
        return c

    lax.fori_loop(1, groups, ask, 0)
    req_in[me] = req_out[me]
    neg_row = lax.rem(neg_v[...], rows_dev)
    neg_hot = hot(jnp.broadcast_to(neg_row, (rows_dev, nneg)) == iota((rows_dev, nneg), 0)).T
    drawn = select_dot(neg_hot, table_v[...])
    mine = rows8(me, nneg)
    panel[mine] = drawn * lax.rsqrt(rows_sum(drawn * drawn) + 1e-06)

    def pass_on(block, device):
        where = rows8(block, nneg)
        remote(panel.at[where], panel.at[where], neg_send, neg_recv.at[block], {"group": device}).start()

    def arrive(block):
        where = rows8(block, nneg)
        remote(panel.at[where], panel.at[where], neg_send, neg_recv.at[block], {"group": me}).wait_recv()

    sibling = at(x, y, 1 - core)

    def along_y(block, up, down):
        if up:
            pass_on(block, at(x, y + 1, core))
        if down:
            pass_on(block, at(x, y - 1, core))
        pass_on(block, at(x + 1, y, core))
        pass_on(block, at(x - 1, y, core))
        pass_on(block, sibling)

    ups, downs = ny // 2, (ny - 1) // 2
    along_y(me, True, True)

    def asked():
        return remote(
            req_out.at[pl.ds(0, groups - 1)], req_in.at[pl.ds(0, groups - 1)], req_sems.at[0], req_sems.at[1], {"group": me}
        )

    asked().wait_recv()

    def widen(g, c):
        expand[rows8(g)] = jnp.broadcast_to(req_in[g], (8, count))
        return c

    lax.fori_loop(0, groups, widen, 0)
    lanes, subs = iota((slots, count), 1), lax.rem(iota((slots, count), 0), 8)
    kept = jnp.where(lanes == lax.rem(subs, 4), expand[...], 0).astype(F32).astype(BF16)
    ones = jnp.ones((count, count), BF16)
    named = jnp.dot(kept, ones, preferred_element_type=F32).astype(jnp.int32)
    fits = named == lanes + 1
    serve = jnp.concatenate([hot(fits & (subs < 4)), hot(fits & (subs >= 4))], axis=1)
    half = width // 2
    stacked = jnp.concatenate([table_v[:, :half], table_v[:, half:]], axis=0)
    served[...] = select_dot(serve, stacked)

    def give(k, c):
        peer = lax.rem(me + k, groups)
        remote(served.at[rows8(peer)], recv.at[rows8(me)], row_sems.at[0], row_sems.at[1], {"group": peer}).start()
        return c

    lax.fori_loop(1, groups, give, 0)
    recv[rows8(me)] = served[rows8(me)]
    for k in range(1, ups + 1):
        block = at(x, y - k, core)
        arrive(block)
        along_y(block, k < ups, False)
        if k <= downs:
            block = at(x, y + k, core)
            arrive(block)
            along_y(block, False, k < downs)
    named_t = lax.dot_general(ones, kept, NT, preferred_element_type=F32).astype(jnp.int32)
    fits_t = named_t == iota((count, slots), 0) + 1
    subs_t = lax.rem(iota((count, slots), 1), 8)
    picks[0] = hot(fits_t & (subs_t < 4))
    picks[1] = hot(fits_t & (subs_t >= 4))
    slot_sub = iota((slots, count), 0)
    place[:, :count] = hot(slot_sub == slot_row)
    place[:, count:] = hot(slot_sub == slot_row + 4)
    for load in loads[3:]:
        load.wait()

    def refine(source, high, low):
        def body(i, c):
            where = rows8(i, 32)
            high[where], low[where] = weights_of(source[where])
            return c

        lax.fori_loop(0, width // 32, body, 0)

    refine(w_in_v, in_hi, in_lo)
    refine(w_out_v, out_hi, out_lo)
    times = jnp.broadcast_to(time_v[...], (count, count))
    gap[...] = jnp.abs(times - times.T)
    buckets = rab_s.shape[1]
    for b in range(4):
        where = slice(b * count // 4, (b + 1) * count // 4)
        gaps = gap[where]

        def look(d, sums):
            for e in range(4):
                here = gaps == d * 4 + e
                sums = tuple(jnp.where(here, rab_s[n, d * 4 + e], s) for n, s in enumerate(sums))
            return sums

        found = lax.fori_loop(0, buckets // 4, look, (jnp.zeros(gaps.shape, F32),) * heads)
        for n in range(heads):
            bias[n, where] = found[n]
    seg_row, seg_col = jnp.zeros((count, count), jnp.int32), jnp.zeros((count, count), jnp.int32)
    place_col = iota((count, 1), 0)
    valid = jnp.ones((count, 1), F32)
    end = 0
    for s in range(len_s.shape[1]):
        end = end + len_s[0, s]
        seg_row += jnp.where(col >= end, 1, 0)
        seg_col += jnp.where(row >= end, 1, 0)
        valid = jnp.where(place_col + 1 == end, 0.0, valid)
    allowed = jnp.where((col <= row) & (seg_row == seg_col), 1.0 / MOST_LEN, 0.0)
    valid = jnp.where(place_col + 1 == count, 0.0, valid)

    def given():
        return remote(
            served.at[pl.ds(0, (groups - 1) * 8)], recv.at[pl.ds(0, (groups - 1) * 8)], row_sems.at[0], row_sems.at[1],
            {"group": me},
        )

    given().wait_recv()
    slot_lane = iota((count, slots), 1)
    for q in range(2):
        emb[:, q * half : (q + 1) * half] = select_dot(hot(slot_lane == slot_col + 4 * q), recv[...])
    e = emb[...]
    e = e - rows_sum(e) / width
    scale1 = lax.rsqrt(rows_sum(e * e) / width + 1e-05)
    norm[...] = e * scale1
    for c in range(4):
        part_c = slice(c * width, (c + 1) * width)
        pre = mul3(norm[...], in_hi[:, part_c], in_lo[:, part_c]) + b_in_v[:, part_c]
        sig = 1.0 / (1.0 + jnp.exp(-pre))
        hid[:, part_c] = pre * sig
        slope[:, part_c] = sig * (1.0 + pre * (1.0 - sig))
    order = [0] + [s * k for k in range(1, ups + 1) for s in (-1, 1) if s < 0 or k <= downs]
    for dy in order:
        for dx in (-1, 1):
            block = at(x + dx, y + dy, core)
            arrive(block)
            if (dy % 2 == 0) == (dx < 0):
                pass_on(block, at(x - dx, y, core))
            pass_on(block, sibling)
    size = width // heads
    root = size ** (-0.5)

    def head(part_c, n):
        return slice(part_c * width + n * size, part_c * width + (n + 1) * size)

    for n in range(heads):
        score = mul3(hid[:, head(2, n)], *weights_of(hid[:, head(3, n)]), NT) * root + bias[n]
        sig = 1.0 / (1.0 + jnp.exp(-score))
        weight = score * sig * allowed
        attn[n] = weight
        attn_slope[n] = sig * (1.0 + score * (1.0 - sig)) * allowed
        mixed[:, head(0, n)] = mul3(weight, *weights_of(hid[:, head(1, n)]))
    for dy in order:
        block = at(x + 2, y + dy, core)
        arrive(block)
        pass_on(block, sibling)
    m = mixed[...]
    m = m - rows_sum(m) / width
    scale2 = lax.rsqrt(rows_sum(m * m) / width + 1e-05)
    mixed[...] = m * scale2
    out = mul3(mixed[...] * hid[:, :width], out_hi[...], out_lo[...]) + emb[...]
    scale3 = lax.rsqrt(rows_sum(out * out) + 1e-06)
    state = out * scale3
    e = emb[...]
    row_col = iota((count, width), 0)
    after = jnp.where(row_col == count - 1, 0.0, pltpu.roll(e, count - 1, 0))
    scale4 = lax.rsqrt(rows_sum(after * after) + 1e-06)
    target = after * scale4
    positive = rows_sum(state * target) / TEMPER
    zneg = jnp.zeros((count, 1), F32)
    pulled = jnp.zeros((count, width), F32)
    state_hi, state_lo = weights_of(state)
    state_two = jnp.concatenate([state_hi, state_lo], axis=0)
    for dx in (0, -1, 1, 2):
        for dy in range(ny):
            arrive(at(x + dx, y + dy, 1 - core))
        block = panel[rows8(lax.rem(x + dx + nx, nx), 2 * ny * nneg)]
        high, low = weights_of(block)
        logit = lax.dot_general(state_two, high, NT, preferred_element_type=F32)
        logit = logit[:count] + logit[count:] + lax.dot_general(state_hi, low, NT, preferred_element_type=F32)
        exps = jnp.exp(logit / TEMPER)
        zneg += rows_sum(exps)
        pulled += mul3(exps, high, low)
    expos = jnp.exp(positive)
    total = expos + zneg
    loss = valid * (jnp.log(total) - positive)
    loss_ref[...] = jnp.broadcast_to(loss, (count, count)).T[:1]
    share = expos / total - 1.0
    weigh = valid / TEMPER
    d_state = weigh * (share * target + pulled / total)
    d_target = (weigh * share) * state
    d_out = scale3 * (d_state - state * rows_sum(state * d_state))
    d_after = scale4 * (d_target - target * rows_sum(target * d_target))
    d_emb = d_out + jnp.where(row_col == 0, 0.0, pltpu.roll(d_after, 1, 0))
    emb[...] = d_emb
    d_gated = mul3(d_out, out_hi[...], out_lo[...], NT)
    dhid[:, :width] = d_gated * mixed[...] * slope[:, :width]
    mixed[...] = norm_back(d_gated * hid[:, :width], mixed[...], scale2)
    for n in range(heads):
        d_mix = mixed[:, head(0, n)]
        weight = attn[n]
        d_weight = mul3(d_mix, *weights_of(hid[:, head(1, n)]), NT)
        d_score = d_weight * attn_slope[n] * root
        mix_hi, mix_lo = weights_of(d_mix)
        dhid[:, head(1, n)] = mul3(weight.T, mix_hi, mix_lo) * slope[:, head(1, n)]
        dhid[:, head(2, n)] = mul3(d_score, *weights_of(hid[:, head(3, n)])) * slope[:, head(2, n)]
        dhid[:, head(3, n)] = mul3(d_score.T, *weights_of(hid[:, head(2, n)])) * slope[:, head(3, n)]
    d_norm = mul3(dhid[:, :width], in_hi[:, :width], in_lo[:, :width], NT)
    for c in range(1, 4):
        part_c = slice(c * width, (c + 1) * width)
        d_norm += mul3(dhid[:, part_c], in_hi[:, part_c], in_lo[:, part_c], NT)
    emb[...] += norm_back(d_norm, norm[...], scale1)
    chunks = outgoing.shape[0]
    for h in range(chunks):
        cols = [slice((2 * h + q) * 128, (2 * h + q + 1) * 128) for q in range(2)]
        outgoing[h] = select_dot(place[...], jnp.concatenate([emb[:, c] for c in cols], axis=0))

        def send(k, c):
            peer = lax.rem(me + k, groups)
            remote(
                outgoing.at[h, rows8(peer)], incoming.at[h, rows8(me)], send_sem.at[h], recv_sem.at[h], {"group": peer}
            ).start()
            return c

        lax.fori_loop(1, groups, send, 0)
        incoming[h, rows8(me)] = outgoing[h, rows8(me)]

    def whole(h):
        where = pl.ds(0, (groups - 1) * 8)
        return remote(outgoing.at[h, where], incoming.at[h, where], send_sem.at[h], recv_sem.at[h], {"group": me})

    for h in range(chunks):
        whole(h).wait_recv()
        spare = part.shape[1] - 2 * 128
        part[h, pl.ds(2 * 128, spare)] = jnp.zeros((spare, 128), F32)
        for q in range(2):
            part[h, pl.ds(q * 128, 128)] = select_dot(picks[q], incoming[h])

        def scatter(k, c):
            peer = lax.rem(my + k, shards)
            remote(part.at[h, rows8(peer, piece)], rsum.at[h, my], rs_send.at[h], rs_recv.at[h], {"shard": peer}).start()
            return c

        lax.fori_loop(1, shards, scatter, 0)
        rsum[h, my] = part[h, rows8(my, piece)]

    def whole_rs(h):
        where = pl.ds(0, shards - 1)
        return remote(rsum.at[h, where], rsum.at[h, where], rs_send.at[h], rs_recv.at[h], {"shard": my})

    own = rows8(my, piece)
    for h in range(chunks):
        whole_rs(h).wait_recv()
        red_ref[h, own] = jnp.sum(rsum[h], axis=0)

        def spread(k, c):
            peer = lax.rem(my + k, shards)
            remote(red_ref.at[h, own], red_ref.at[h, own], ag_send.at[h], ag_recv.at[h], {"shard": peer}).start()
            return c

        lax.fori_loop(1, shards, spread, 0)
    for h in range(chunks):
        where = pl.ds(0, (shards - 1) * piece)
        tail = remote(red_ref.at[h, where], red_ref.at[h, where], ag_send.at[h], ag_recv.at[h], {"shard": my})
        tail.wait_recv()
        tail.wait_send()
        whole(h).wait_send()
        whole_rs(h).wait_send()
    asked().wait_send()
    given().wait_send()
    sent = pl.ds(0, (groups - 1) * nneg)
    remote(panel.at[sent], panel.at[sent], neg_send, neg_recv.at[0], {"group": me}).wait_send()


def body(item_ids, seq_lengths, time_buckets, neg_ids, table, w_in, b_in, w_out, rab):
    groups, shards = lax.axis_size("group"), lax.axis_size("shard")
    count, width = item_ids.shape[0], table.shape[1]
    heads, hidden = rab.shape[0], w_in.shape[1]
    nneg = neg_ids.shape[1]
    slots, chunks = groups * 8, width // 256
    piece = (-(-256 // shards) + 7) // 8 * 8
    red_rows = shards * piece
    vm, smem, dma, i32 = pltpu.VMEM, pltpu.SMEM, pltpu.SemaphoreType.DMA, jnp.int32
    anywhere = pl.BlockSpec(memory_space=pl.ANY)
    red, loss = pl.pallas_call(
        functools.partial(step_kernel, (groups // 16, 8), shards, piece, heads),
        out_shape=(
            jax.ShapeDtypeStruct((chunks, red_rows, 128), F32),
            jax.ShapeDtypeStruct((1, count), F32),
        ),
        in_specs=[anywhere] * 9,
        out_specs=(pl.BlockSpec(memory_space=vm),) * 2,
        scratch_shapes=[
            vm((1, count), i32),
            smem(seq_lengths.shape, i32),
            vm((1, count), i32),
            vm((1, nneg), i32),
            vm(table.shape, F32),
            vm(w_in.shape, F32),
            vm((1, hidden), F32),
            vm(w_out.shape, F32),
            smem(rab.shape, F32),
            dma((9,)),
            vm(w_in.shape, BF16),
            vm(w_in.shape, BF16),
            vm(w_out.shape, BF16),
            vm(w_out.shape, BF16),
            vm((groups * nneg, width), F32),
            vm((groups, 1, count), i32),
            vm((groups, 1, count), i32),
            vm((slots, count), i32),
            vm((slots, width // 2), F32),
            vm((slots, width // 2), F32),
            vm((slots, 2 * count), BF16),
            vm((2, count, slots), BF16),
            vm((count, width), F32),
            vm((count, width), F32),
            vm((count, hidden), F32),
            vm((count, hidden), F32),
            vm((count, count), i32),
            vm((heads, count, count), F32),
            vm((heads, count, count), F32),
            vm((heads, count, count), F32),
            vm((count, width), F32),
            vm((count, hidden), F32),
            vm((chunks, slots, 128), F32),
            vm((chunks, slots, 128), F32),
            vm((chunks, red_rows, 128), F32),
            vm((chunks, shards, piece, 128), F32),
            dma((2,)),
            dma((2,)),
            dma,
            dma((groups,)),
        ]
        + [dma((chunks,))] * 6,
        compiler_params=pltpu.CompilerParams(collective_id=0, has_side_effects=True, vmem_limit_bytes=56 << 20),
        name="hstu_step",
    )(
        item_ids.reshape(1, -1), seq_lengths, time_buckets.reshape(1, -1), neg_ids, table, w_in, b_in.reshape(1, -1), w_out,
        rab,
    )
    parts = red[:, :256].reshape(chunks * 2, count, 128)
    return parts.transpose(1, 0, 2).reshape(count, width), loss.reshape(-1)


def solution(mesh):
    in_specs = (
        P(("shard", "group")),
        P(("shard", "group"), None),
        P(("shard", "group")),
        P("shard", "group"),
        P("group", None),
        P(),
        P(),
        P(),
        P(),
    )
    out_specs = (P("group", None), P(("shard", "group")))
    return jax.shard_map(body, mesh=mesh, in_specs=in_specs, out_specs=out_specs, check_vma=False)
```

time: 279 us -> 104 us (0.37)
  the two profiles are of different devices: /device:TPU:2 before, /device:TPU:1 now
where the time goes in v2:
time: 104 us
  Pallas kernels  101 us (97%)
  local copies, waits for them, and re-layouts  2.89 us (3%)
    pallas_call x1, Pallas kernels, body(): pl.pallas_call(functools.partial(step_kernel, (groups // 16, 8), shards,...  101 us

profile of v2, /device:TPU:1, one launch (start us, length us, event | category | flops | bytes accessed | tf_op | source)
XLA Modules:
  0.0 104.3 jit_solution(16992249624142767996)
XLA Ops:
  0.6 100.8 %hstu_step.1 = (f32[2,288,128]{2,1,0:T(8,128)}, f32[1,128]{1,0:T(1,128)}) custom-call(s32[1,128]{1,0:T(1,128)} %bitcast.14, s32[1,8]{1,0:T(1,128)} %len_h.1, s32[1,128]{1,0:T(1,128)} %bitcast.15, s32[1,32]{1,0:T(1,128)} %neg_h.1, f32[128,512]{1,0:T(8,128)} %table_h.1, f32[512,2048]{1,0:T(8,128)} %w_in_h.1, f32[1,2048]{1,0:T(1,128)} %bitcast.13, ...), custom_call_target="tpu_custom_call" | custom-call | tf_op jit(solution)/shard_map/hstu_step/pallas_call | solution.py:435
  101.4 1.0 slice.3
  102.4 0.7 copy.14
  103.1 1.2 %copy.16 = f32[128]{0:T(128)} copy(f32[128]{0:T(128)} %bitcast.16) | data formatting | bytes 1024

commit v3 on v2

--- a/solution.py
+++ b/solution.py
@@ -80,10 +80,10 @@
     red_ref, loss_ref,
     ids_v, len_s, time_v, neg_v, table_v, w_in_v, b_in_v, w_out_v, rab_s, load_sems,
     in_hi, in_lo, out_hi, out_lo, panel,
-    req_out, req_in, expand, served, recv, place, picks,
+    ids_all, expand, served, recv, place, picks,
     emb, norm, hid, slope, gap, bias, attn, attn_slope, mixed, dhid,
     outgoing, incoming, part, rsum,
-    req_sems, row_sems, neg_send, neg_recv, send_sem, recv_sem, rs_send, rs_recv, ag_send, ag_recv,
+    id_sems, row_sems, neg_send, neg_recv, send_sem, recv_sem, rs_send, rs_recv, ag_send, ag_recv,
 ):
     nx, ny = dims
     groups = nx * ny * 2
@@ -119,32 +119,23 @@
 
     lax.fori_loop(1, shards, hello_z, 0)
     loads[0].wait()
-    ids = jnp.broadcast_to(ids_v[...], (count, count))
-    ids_t = ids.T
     rows_dev = table_v.shape[0]
-    own_row, own_col = ids // rows_dev, ids_t // rows_dev
-    same = own_row == own_col
-    col, row = iota((count, count), 1), iota((count, count), 0)
-    rank_col = jnp.sum(jnp.where(same & (col < row), 1, 0), axis=1, keepdims=True)
-    rank_row = jnp.sum(jnp.where(same & (row < col), 1, 0), axis=0, keepdims=True)
-    slot_col = own_col[:, :1] * 8 + rank_col
-    slot_row = own_row[:1] * 8 + rank_row
-    owner_hot = hot(jnp.broadcast_to(own_row[:1], (groups, count)) == iota((groups, count), 0))
-    wanted = jnp.where(lax.rem(col, 4) == rank_col, ids_t - own_col * rows_dev + 1, 0)
-    requests = jnp.dot(owner_hot, wanted.astype(F32).astype(BF16), preferred_element_type=F32)
-    for g in range(groups):
-        req_out[g] = requests[g : g + 1].astype(jnp.int32)
+    ids_all[me] = ids_v[...]
+    pl.semaphore_wait(barrier, groups - 1 + shards - 1)
+
+    def fold(i, n):
+        return jnp.where(lax.rem(i, 2) == 1, n // 2 - (i + 1) // 2, n // 2 + i // 2)
+
+    def nth_peer(k):
+        return at(x + fold(lax.rem(k, 2 * nx) // 2, nx), y + fold(k // (2 * nx), ny), lax.rem(core + 1 - lax.rem(k, 2), 2))
+
+    def tell(k, c):
+        remote(ids_all.at[me], ids_all.at[me], id_sems.at[0], id_sems.at[1], {"group": nth_peer(k)}).start()
+        return c
+
+    lax.fori_loop(0, groups - 1, tell, 0)
     loads[1].wait()
     loads[2].wait()
-    pl.semaphore_wait(barrier, groups - 1 + shards - 1)
-
-    def ask(k, c):
-        peer = lax.rem(me + k, groups)
-        remote(req_out.at[peer], req_in.at[me], req_sems.at[0], req_sems.at[1], {"group": peer}).start()
-        return c
-
-    lax.fori_loop(1, groups, ask, 0)
-    req_in[me] = req_out[me]
     neg_row = lax.rem(neg_v[...], rows_dev)
     neg_hot = hot(jnp.broadcast_to(neg_row, (rows_dev, nneg)) == iota((rows_dev, nneg), 0)).T
     drawn = select_dot(neg_hot, table_v[...])
@@ -161,32 +152,51 @@
 
     sibling = at(x, y, 1 - core)
 
-    def along_y(block, up, down):
-        if up:
-            pass_on(block, at(x, y + 1, core))
-        if down:
-            pass_on(block, at(x, y - 1, core))
+    def across_x(block):
         pass_on(block, at(x + 1, y, core))
         pass_on(block, at(x - 1, y, core))
+
+    pass_on(me, at(x, y + 1, core))
+    pass_on(me, at(x, y - 1, core))
+
+    def told():
+        where = pl.ds(0, groups - 1)
+        return remote(ids_all.at[where], ids_all.at[where], id_sems.at[0], id_sems.at[1], {"group": me})
+
+    across_x(me)
+    pass_on(me, sibling)
+    ups, downs = ny // 2, (ny - 1) // 2
+
+    def step_y(k):
+        block = at(x, y - k, core)
+        arrive(block)
+        if k < ups:
+            pass_on(block, at(x, y + 1, core))
+        across_x(block)
         pass_on(block, sibling)
-
-    ups, downs = ny // 2, (ny - 1) // 2
-    along_y(me, True, True)
-
-    def asked():
-        return remote(
-            req_out.at[pl.ds(0, groups - 1)], req_in.at[pl.ds(0, groups - 1)], req_sems.at[0], req_sems.at[1], {"group": me}
-        )
-
-    asked().wait_recv()
+        if k <= downs:
+            block = at(x, y + k, core)
+            arrive(block)
+            if k < downs:
+                pass_on(block, at(x, y - 1, core))
+            across_x(block)
+            pass_on(block, sibling)
+
+    step_y(1)
+    told().wait_recv()
 
     def widen(g, c):
-        expand[rows8(g)] = jnp.broadcast_to(req_in[g], (8, count))
+        expand[rows8(g)] = jnp.broadcast_to(ids_all[g], (8, count))
         return c
 
     lax.fori_loop(0, groups, widen, 0)
+    col, row = iota((count, count), 1), iota((count, count), 0)
     lanes, subs = iota((slots, count), 1), lax.rem(iota((slots, count), 0), 8)
-    kept = jnp.where(lanes == lax.rem(subs, 4), expand[...], 0).astype(F32).astype(BF16)
+    asked = expand[...]
+    here = asked // rows_dev == me
+    earlier = hot(row < col)
+    turn = jnp.dot(hot(here), earlier, preferred_element_type=F32).astype(jnp.int32)
+    kept = jnp.where(here & (turn == lax.rem(subs, 4)), asked - me * rows_dev + 1, 0).astype(F32).astype(BF16)
     ones = jnp.ones((count, count), BF16)
     named = jnp.dot(kept, ones, preferred_element_type=F32).astype(jnp.int32)
     fits = named == lanes + 1
@@ -196,20 +206,33 @@
     served[...] = select_dot(serve, stacked)
 
     def give(k, c):
-        peer = lax.rem(me + k, groups)
+        peer = nth_peer(k)
         remote(served.at[rows8(peer)], recv.at[rows8(me)], row_sems.at[0], row_sems.at[1], {"group": peer}).start()
         return c
 
-    lax.fori_loop(1, groups, give, 0)
     recv[rows8(me)] = served[rows8(me)]
-    for k in range(1, ups + 1):
-        block = at(x, y - k, core)
-        arrive(block)
-        along_y(block, k < ups, False)
-        if k <= downs:
-            block = at(x, y + k, core)
+    for k in range(2, ups + 1):
+        lax.fori_loop((groups - 1) * (k - 2) // (ups - 1), (groups - 1) * (k - 1) // (ups - 1), give, 0)
+        step_y(k)
+    order = [0] + [s * k for k in range(1, ups + 1) for s in (-1, 1) if s < 0 or k <= downs]
+
+    def step_x(dy):
+        for dx in (-1, 1):
+            block = at(x + dx, y + dy, core)
             arrive(block)
-            along_y(block, False, k < downs)
+            if (dy % 2 == 0) == (dx < 0):
+                pass_on(block, at(x - dx, y, core))
+            pass_on(block, sibling)
+
+    step_x(order[0])
+    ids = jnp.broadcast_to(ids_v[...], (count, count))
+    ids_t = ids.T
+    own_row, own_col = ids // rows_dev, ids_t // rows_dev
+    same = own_row == own_col
+    rank_col = jnp.sum(jnp.where(same & (col < row), 1, 0), axis=1, keepdims=True)
+    rank_row = jnp.sum(jnp.where(same & (row < col), 1, 0), axis=0, keepdims=True)
+    slot_col = own_col[:, :1] * 8 + rank_col
+    slot_row = own_row[:1] * 8 + rank_row
     named_t = lax.dot_general(ones, kept, NT, preferred_element_type=F32).astype(jnp.int32)
     fits_t = named_t == iota((count, slots), 0) + 1
     subs_t = lax.rem(iota((count, slots), 1), 8)
@@ -220,6 +243,7 @@
     place[:, count:] = hot(slot_sub == slot_row + 4)
     for load in loads[3:]:
         load.wait()
+    step_x(order[1])
 
     def refine(source, high, low):
         def body(i, c):
@@ -230,6 +254,7 @@
         lax.fori_loop(0, width // 32, body, 0)
 
     refine(w_in_v, in_hi, in_lo)
+    step_x(order[2])
     refine(w_out_v, out_hi, out_lo)
     times = jnp.broadcast_to(time_v[...], (count, count))
     gap[...] = jnp.abs(times - times.T)
@@ -247,6 +272,7 @@
         found = lax.fori_loop(0, buckets // 4, look, (jnp.zeros(gaps.shape, F32),) * heads)
         for n in range(heads):
             bias[n, where] = found[n]
+        step_x(order[3 + b])
     seg_row, seg_col = jnp.zeros((count, count), jnp.int32), jnp.zeros((count, count), jnp.int32)
     place_col = iota((count, 1), 0)
     valid = jnp.ones((count, 1), F32)
@@ -258,6 +284,9 @@
         valid = jnp.where(place_col + 1 == end, 0.0, valid)
     allowed = jnp.where((col <= row) & (seg_row == seg_col), 1.0 / MOST_LEN, 0.0)
     valid = jnp.where(place_col + 1 == count, 0.0, valid)
+
+    for dy in order[7:]:
+        step_x(dy)
 
     def given():
         return remote(
@@ -279,14 +308,10 @@
         sig = 1.0 / (1.0 + jnp.exp(-pre))
         hid[:, part_c] = pre * sig
         slope[:, part_c] = sig * (1.0 + pre * (1.0 - sig))
-    order = [0] + [s * k for k in range(1, ups + 1) for s in (-1, 1) if s < 0 or k <= downs]
     for dy in order:
-        for dx in (-1, 1):
-            block = at(x + dx, y + dy, core)
-            arrive(block)
-            if (dy % 2 == 0) == (dx < 0):
-                pass_on(block, at(x - dx, y, core))
-            pass_on(block, sibling)
+        block = at(x + 2, y + dy, core)
+        arrive(block)
+        pass_on(block, sibling)
     size = width // heads
     root = size ** (-0.5)
 
@@ -300,10 +325,6 @@
         attn[n] = weight
         attn_slope[n] = sig * (1.0 + score * (1.0 - sig)) * allowed
         mixed[:, head(0, n)] = mul3(weight, *weights_of(hid[:, head(1, n)]))
-    for dy in order:
-        block = at(x + 2, y + dy, core)
-        arrive(block)
-        pass_on(block, sibling)
     m = mixed[...]
     m = m - rows_sum(m) / width
     scale2 = lax.rsqrt(rows_sum(m * m) / width + 1e-05)
@@ -361,18 +382,19 @@
         d_norm += mul3(dhid[:, part_c], in_hi[:, part_c], in_lo[:, part_c], NT)
     emb[...] += norm_back(d_norm, norm[...], scale1)
     chunks = outgoing.shape[0]
+    z_order = sorted(range(1, shards), key=lambda k: -min(k, shards - k))
     for h in range(chunks):
         cols = [slice((2 * h + q) * 128, (2 * h + q + 1) * 128) for q in range(2)]
         outgoing[h] = select_dot(place[...], jnp.concatenate([emb[:, c] for c in cols], axis=0))
 
         def send(k, c):
-            peer = lax.rem(me + k, groups)
+            peer = nth_peer(k)
             remote(
                 outgoing.at[h, rows8(peer)], incoming.at[h, rows8(me)], send_sem.at[h], recv_sem.at[h], {"group": peer}
             ).start()
             return c
 
-        lax.fori_loop(1, groups, send, 0)
+        lax.fori_loop(0, groups - 1, send, 0)
         incoming[h, rows8(me)] = outgoing[h, rows8(me)]
 
     def whole(h):
@@ -386,12 +408,9 @@
         for q in range(2):
             part[h, pl.ds(q * 128, 128)] = select_dot(picks[q], incoming[h])
 
-        def scatter(k, c):
+        for k in z_order:
             peer = lax.rem(my + k, shards)
             remote(part.at[h, rows8(peer, piece)], rsum.at[h, my], rs_send.at[h], rs_recv.at[h], {"shard": peer}).start()
-            return c
-
-        lax.fori_loop(1, shards, scatter, 0)
         rsum[h, my] = part[h, rows8(my, piece)]
 
     def whole_rs(h):
@@ -403,12 +422,9 @@
         whole_rs(h).wait_recv()
         red_ref[h, own] = jnp.sum(rsum[h], axis=0)
 
-        def spread(k, c):
+        for k in z_order:
             peer = lax.rem(my + k, shards)
             remote(red_ref.at[h, own], red_ref.at[h, own], ag_send.at[h], ag_recv.at[h], {"shard": peer}).start()
-            return c
-
-        lax.fori_loop(1, shards, spread, 0)
     for h in range(chunks):
         where = pl.ds(0, (shards - 1) * piece)
         tail = remote(red_ref.at[h, where], red_ref.at[h, where], ag_send.at[h], ag_recv.at[h], {"shard": my})
@@ -416,7 +432,7 @@
         tail.wait_send()
         whole(h).wait_send()
         whole_rs(h).wait_send()
-    asked().wait_send()
+    told().wait_send()
     given().wait_send()
     sent = pl.ds(0, (groups - 1) * nneg)
     remote(panel.at[sent], panel.at[sent], neg_send, neg_recv.at[0], {"group": me}).wait_send()
@@ -457,7 +473,6 @@
             vm(w_out.shape, BF16),
             vm((groups * nneg, width), F32),
             vm((groups, 1, count), i32),
-            vm((groups, 1, count), i32),
             vm((slots, count), i32),
             vm((slots, width // 2), F32),
             vm((slots, width // 2), F32),

time: 104 us -> 97.2 us (0.935)
  Pallas kernels: 101 us -> 93.5 us
    pallas_call x1, Pallas kernels: 101 us -> 93.5 us  [body(): pl.pallas_call(functools.partial(step_kernel, (groups // 16, 8), shards,...]
where the time goes in v3:
time: 97.2 us; the launch traced here: 97.1 us
  Pallas kernels  93.5 us (96%)
  local copies, waits for them, and re-layouts  2.89 us (3%)
    pallas_call x1, Pallas kernels, body(): pl.pallas_call(functools.partial(step_kernel, (groups // 16, 8), shards,...  93.5 us

profile of v3, /device:TPU:1, one launch (start us, length us, event | category | flops | bytes accessed | tf_op | source)
XLA Modules:
  0.0 97.1 jit_solution(15409051936809598731)
XLA Ops:
  0.6 93.5 %hstu_step.1 = (f32[2,288,128]{2,1,0:T(8,128)}, f32[1,128]{1,0:T(1,128)}) custom-call(s32[1,128]{1,0:T(1,128)} %bitcast.14, s32[1,8]{1,0:T(1,128)} %len_h.1, s32[1,128]{1,0:T(1,128)} %bitcast.15, s32[1,32]{1,0:T(1,128)} %neg_h.1, f32[128,512]{1,0:T(8,128)} %table_h.1, f32[512,2048]{1,0:T(8,128)} %w_in_h.1, f32[1,2048]{1,0:T(1,128)} %bitcast.13, ...), custom_call_target="tpu_custom_call" | custom-call | tf_op jit(solution)/shard_map/hstu_step/pallas_call | solution.py:451
  94.2 1.0 %slice.3 = f32[2,256,128]{2,1,0:T(8,128)S(1)} slice(f32[2,288,128]{2,1,0:T(8,128)} %get-tuple-element.4), slice={[0:2], [0:256], [0:128]} | slice | bytes 524288 | tf_op jit(solution)/shard_map/slice | solution.py:507
  95.1 0.7 copy.14
  95.9 1.2 %copy.16 = f32[128]{0:T(128)} copy(f32[128]{0:T(128)} %bitcast.16) | data formatting | bytes 1024

commit v4 on v3

--- a/solution.py
+++ b/solution.py
@@ -156,8 +156,8 @@
         pass_on(block, at(x + 1, y, core))
         pass_on(block, at(x - 1, y, core))
 
-    pass_on(me, at(x, y + 1, core))
-    pass_on(me, at(x, y - 1, core))
+    for dy in (1, -1, 2, -2):
+        pass_on(me, at(x, y + dy, core))
 
     def told():
         where = pl.ds(0, groups - 1)
@@ -165,24 +165,18 @@
 
     across_x(me)
     pass_on(me, sibling)
-    ups, downs = ny // 2, (ny - 1) // 2
-
-    def step_y(k):
-        block = at(x, y - k, core)
+    def step_y(dy, onward=()):
+        block = at(x, y + dy, core)
         arrive(block)
-        if k < ups:
-            pass_on(block, at(x, y + 1, core))
+        for to in onward:
+            pass_on(block, at(x, y + to, core))
         across_x(block)
         pass_on(block, sibling)
-        if k <= downs:
-            block = at(x, y + k, core)
-            arrive(block)
-            if k < downs:
-                pass_on(block, at(x, y - 1, core))
-            across_x(block)
-            pass_on(block, sibling)
-
+
+    step_y(-1)
     step_y(1)
+    step_y(-2, (2, 1))
+    step_y(2, (-1,))
     told().wait_recv()
 
     def widen(g, c):
@@ -211,10 +205,10 @@
         return c
 
     recv[rows8(me)] = served[rows8(me)]
-    for k in range(2, ups + 1):
-        lax.fori_loop((groups - 1) * (k - 2) // (ups - 1), (groups - 1) * (k - 1) // (ups - 1), give, 0)
-        step_y(k)
-    order = [0] + [s * k for k in range(1, ups + 1) for s in (-1, 1) if s < 0 or k <= downs]
+    lax.fori_loop(0, groups - 1, give, 0)
+    for dy in (-3, 3, -4):
+        step_y(dy)
+    order = [0, -1, 1, -2, 2, -3, 3, -4]
 
     def step_x(dy):
         for dx in (-1, 1):
@@ -382,6 +376,7 @@
         d_norm += mul3(dhid[:, part_c], in_hi[:, part_c], in_lo[:, part_c], NT)
     emb[...] += norm_back(d_norm, norm[...], scale1)
     chunks = outgoing.shape[0]
+    last = shards - 1
     z_order = sorted(range(1, shards), key=lambda k: -min(k, shards - k))
     for h in range(chunks):
         cols = [slice((2 * h + q) * 128, (2 * h + q + 1) * 128) for q in range(2)]
@@ -410,28 +405,48 @@
 
         for k in z_order:
             peer = lax.rem(my + k, shards)
-            remote(part.at[h, rows8(peer, piece)], rsum.at[h, my], rs_send.at[h], rs_recv.at[h], {"shard": peer}).start()
+
+            @pl.when(peer != last)
+            def _():
+                remote(
+                    part.at[h, rows8(peer, piece)], rsum.at[h, my], rs_send.at[h], rs_recv.at[h], {"shard": peer}
+                ).start()
+
         rsum[h, my] = part[h, rows8(my, piece)]
 
-    def whole_rs(h):
-        where = pl.ds(0, shards - 1)
+    def some_rs(h, pieces):
+        where = pl.ds(0, pieces)
         return remote(rsum.at[h, where], rsum.at[h, where], rs_send.at[h], rs_recv.at[h], {"shard": my})
+
+    def some_red(h, pieces):
+        where = pl.ds(0, pieces * piece)
+        return remote(red_ref.at[h, where], red_ref.at[h, where], ag_send.at[h], ag_recv.at[h], {"shard": my})
 
     own = rows8(my, piece)
     for h in range(chunks):
-        whole_rs(h).wait_recv()
-        red_ref[h, own] = jnp.sum(rsum[h], axis=0)
-
-        for k in z_order:
-            peer = lax.rem(my + k, shards)
-            remote(red_ref.at[h, own], red_ref.at[h, own], ag_send.at[h], ag_recv.at[h], {"shard": peer}).start()
+
+        @pl.when(my != last)
+        def _():
+            some_rs(h, shards - 1).wait_recv()
+            red_ref[h, own] = jnp.sum(rsum[h], axis=0)
+            for k in z_order:
+                peer = lax.rem(my + k, shards)
+                remote(red_ref.at[h, own], red_ref.at[h, own], ag_send.at[h], ag_recv.at[h], {"shard": peer}).start()
+
     for h in range(chunks):
-        where = pl.ds(0, (shards - 1) * piece)
-        tail = remote(red_ref.at[h, where], red_ref.at[h, where], ag_send.at[h], ag_recv.at[h], {"shard": my})
-        tail.wait_recv()
-        tail.wait_send()
+
+        @pl.when(my != last)
+        def _():
+            some_red(h, shards - 2).wait_recv()
+            some_red(h, shards - 1).wait_send()
+            some_rs(h, shards - 2).wait_send()
+
+        @pl.when(my == last)
+        def _():
+            some_red(h, shards - 1).wait_recv()
+            some_rs(h, shards - 1).wait_send()
+
         whole(h).wait_send()
-        whole_rs(h).wait_send()
     told().wait_send()
     given().wait_send()
     sent = pl.ds(0, (groups - 1) * nneg)

time: 97.2 us -> 95.4 us (0.981)
  Pallas kernels: 93.5 us -> 91.7 us
    pallas_call x1, Pallas kernels: 93.5 us -> 91.7 us  [body(): pl.pallas_call(functools.partial(step_kernel, (groups // 16, 8), shards,...]
where the time goes in v4:
time: 95.4 us; the launch traced here: 95.2 us
  Pallas kernels  91.7 us (96%)
  local copies, waits for them, and re-layouts  2.89 us (3%)
    pallas_call x1, Pallas kernels, body(): pl.pallas_call(functools.partial(step_kernel, (groups // 16, 8), shards,...  91.7 us

profile of v4, /device:TPU:1, one launch (start us, length us, event | category | flops | bytes accessed | tf_op | source)
XLA Modules:
  0.0 95.2 jit_solution(3088044601770215234)
XLA Ops:
  0.6 91.7 %hstu_step.1 = (f32[2,288,128]{2,1,0:T(8,128)}, f32[1,128]{1,0:T(1,128)}) custom-call(s32[1,128]{1,0:T(1,128)} %bitcast.14, s32[1,8]{1,0:T(1,128)} %len_h.1, s32[1,128]{1,0:T(1,128)} %bitcast.15, s32[1,32]{1,0:T(1,128)} %neg_h.1, f32[128,512]{1,0:T(8,128)} %table_h.1, f32[512,2048]{1,0:T(8,128)} %w_in_h.1, f32[1,2048]{1,0:T(1,128)} %bitcast.13, ...), custom_call_target="tpu_custom_call" | custom-call | tf_op jit(solution)/shard_map/hstu_step/pallas_call | solution.py:466
  92.3 1.0 %slice.3 = f32[2,256,128]{2,1,0:T(8,128)S(1)} slice(f32[2,288,128]{2,1,0:T(8,128)} %get-tuple-element.4), slice={[0:2], [0:256], [0:128]} | slice | bytes 524288 | tf_op jit(solution)/shard_map/slice | solution.py:522
  93.3 0.7 copy.14
  94.0 1.2 %copy.16 = f32[128]{0:T(128)} copy(f32[128]{0:T(128)} %bitcast.16) | data formatting | bytes 1024

commit v5 on v4

--- a/solution.py
+++ b/solution.py
@@ -453,6 +453,13 @@
     remote(panel.at[sent], panel.at[sent], neg_send, neg_recv.at[0], {"group": me}).wait_send()
 
 
+def settle_kernel(red_ref, loss_in, grad_ref, loss_ref):
+    count = grad_ref.shape[0]
+    for q in range(grad_ref.shape[1] // 128):
+        grad_ref[:, q * 128 : (q + 1) * 128] = red_ref[q // 2, q % 2 * count : (q % 2 + 1) * count]
+    loss_ref[...] = loss_in[...]
+
+
 def body(item_ids, seq_lengths, time_buckets, neg_ids, table, w_in, b_in, w_out, rab):
     groups, shards = lax.axis_size("group"), lax.axis_size("shard")
     count, width = item_ids.shape[0], table.shape[1]
@@ -519,8 +526,15 @@
         item_ids.reshape(1, -1), seq_lengths, time_buckets.reshape(1, -1), neg_ids, table, w_in, b_in.reshape(1, -1), w_out,
         rab,
     )
-    parts = red[:, :256].reshape(chunks * 2, count, 128)
-    return parts.transpose(1, 0, 2).reshape(count, width), loss.reshape(-1)
+    inside = pl.BlockSpec(memory_space=vm)
+    grad, loss = pl.pallas_call(
+        settle_kernel,
+        out_shape=(jax.ShapeDtypeStruct((count, width), F32), jax.ShapeDtypeStruct((1, count), F32)),
+        in_specs=[inside] * 2,
+        out_specs=(inside,) * 2,
+        name="settle",
+    )(red, loss)
+    return grad, loss.reshape(-1)
 
 
 def solution(mesh):

time: 95.4 us -> 94.2 us (0.987)
  local copies, waits for them, and re-layouts: 2.89 us -> 0 us
  Pallas kernels: 91.7 us -> 93.4 us
    pallas_call x0 -> x1, Pallas kernels: none -> 1.7 us  [body(): pl.pallas_call(settle_kernel, out_shape=(jax.ShapeDtypeStruct((count, wid...]
    unnamed x1 -> x0, local copies, waits for them, and re-layouts: 1.19 us -> none
    slice x1 -> x0, local copies, waits for them, and re-layouts: 0.97 us -> none  [body(): parts = red[:, :256].reshape(chunks * 2, count, 128)]
where the time goes in v5:
time: 94.2 us; the launch traced here: 94 us
  Pallas kernels  93.4 us (99%)
    pallas_call x1, Pallas kernels, body(): pl.pallas_call(functools.partial(step_kernel, (groups // 16, 8), shards,...  91.7 us

profile of v5, /device:TPU:1, one launch (start us, length us, event | category | flops | bytes accessed | tf_op | source)
XLA Modules:
  0.0 94.0 jit_solution(13366171120918810344)
XLA Ops:
  0.6 91.7 %hstu_step.1 = (f32[2,288,128]{2,1,0:T(8,128)}, f32[1,128]{1,0:T(1,128)}) custom-call(s32[1,128]{1,0:T(1,128)} %bitcast.5, s32[1,8]{1,0:T(1,128)} %len_h.1, s32[1,128]{1,0:T(1,128)} %bitcast.6, s32[1,32]{1,0:T(1,128)} %neg_h.1, f32[128,512]{1,0:T(8,128)} %table_h.1, f32[512,2048]{1,0:T(8,128)} %w_in_h.1, f32[1,2048]{1,0:T(1,128)} %bitcast.4, ...), custom_call_target="tpu_custom_call" | custom-call | tf_op jit(solution)/shard_map/hstu_step/pallas_call | solution.py:473
  92.3 1.7 %settle.1 = (f32[128,512]{1,0:T(8,128)}, f32[1,128]{1,0:T(1,128)}) custom-call(f32[2,288,128]{2,1,0:T(8,128)} %get-tuple-element.6.red_ref, f32[1,128]{1,0:T(1,128)} %get-tuple-element.7.loss_in), custom_call_target="tpu_custom_call" | custom-call | tf_op jit(solution)/shard_map/settle/pallas_call | solution.py:530
